TPU v7x, 512 devices: a whole 4x4x16 slice. The times are simulated.
512 devices in a mesh: dp: 16 (over z_hi, y), tensor: 32 (over z_lo, x, core).
Axes of the slice: x: 4, y: 4, z: 16 (z_hi: 4, z_lo: 4; z = z_hi * 4 + z_lo), core: 2. Of those that a mesh axis runs over, the one named last changes fastest.
Arguments:
- hidden: bfloat16 [1024, 32, 28672], P('dp', None, 'tensor'), may hold values from -6 to 6
- out_grad: bfloat16 [1024, 32, 8192], P('dp', None, 'tensor'), may hold values from -6 to 6
- proj_in: bfloat16 [28672, 64], P('tensor'), may hold values from -0.03125 to 0.03125
- proj_out: bfloat16 [8192, 64], P('tensor'), may hold values from -0.0625 to 0.0625
- lengths: int32 [1024], P('dp'), may hold values from 1 to 32, 16384 in all
- task_ids: int32 [16], replicated, may hold values from 0 to 1
Outputs:
- similarity: float32 [1024, 16, 64], P('dp', None, 'tensor')
Inputs may be any that keep to these rules, and one draw needn't show every extreme that they name: `lengths`: at least one sequence is exactly 32 long.
All inputs are finite; a program needn't handle non-finite values. No bound on the sum of `lengths` on one device may be relied on, other than what follows from the above.
Results may differ from a plain program's by a relative error of at most 0.0003.
Values sent between devices are 32-bit elements; how exact they have to be, the bound alone decides.
No kernel may reach another device: no remote copies, remote signals or barrier semaphores. Data moves between devices by JAX's collectives and lax.ppermute only.
A program may use at most 64 MiB of HBM per device.

v0:
```python
import jax
import jax.numpy as jnp
from jax import lax
from jax.sharding import PartitionSpec as P

epsilon = 1e-06


def from_behind(value, axis, steps):
    count = lax.axis_size(axis)
    pairs = [(source, (source + steps) % count) for source in range(count)]
    return lax.ppermute(value, axis, pairs)


def normalized(summed, lengths):
    seq_count, seq_len, doubled = summed.shape
    width_low = doubled // 2
    live_mask = (jnp.arange(seq_len, dtype=jnp.int32)[None, :] < lengths[:, None]).astype(
        jnp.float32
    )
    inputs_low = summed[:, :, :width_low] * live_mask[:, :, None]
    outputs_low = summed[:, :, width_low:]
    sketch = jnp.einsum("slk,slm->skm", inputs_low, outputs_low, precision=lax.Precision.HIGHEST)
    flattened = sketch.reshape(seq_count, width_low * width_low)
    root_mean = jnp.sqrt(jnp.mean(flattened * flattened, axis=1, keepdims=True) + epsilon)
    return flattened / root_mean


def inner_rows(left, right):
    return lax.dot_general(
        left,
        right,
        (((1,), (1,)), ((), ())),
        preferred_element_type=jnp.float32,
        precision=lax.Precision.HIGHEST,
    )


def body(hidden, out_grad, proj_in, proj_out, lengths, task_ids):
    block_rows, seq_len, _ = hidden.shape
    groups = lax.axis_size("dp")
    slices = lax.axis_size("tensor")
    share_rows = block_rows // slices
    group_index = lax.axis_index("dp")
    slice_index = lax.axis_index("tensor")
    width_low = proj_in.shape[1]
    factor = 1.0 / width_low
    inputs_part = jnp.dot(
        hidden.reshape(block_rows * seq_len, -1), proj_in, preferred_element_type=jnp.float32
    )
    outputs_part = jnp.dot(
        out_grad.reshape(block_rows * seq_len, -1), proj_out, preferred_element_type=jnp.float32
    )
    partial_value = jnp.concatenate([inputs_part, outputs_part], axis=1).reshape(
        block_rows, seq_len, 2 * width_low
    )
    summed = lax.psum(partial_value, "tensor")
    own_block = normalized(summed, lengths)
    mine = lax.dynamic_slice_in_dim(own_block, slice_index * share_rows, share_rows, 0)
    block_ids = jnp.arange(groups, dtype=jnp.int32)
    own_task = jnp.sum(jnp.where(block_ids == group_index, task_ids, 0))

    def place(result, visiting, source):
        source_task = jnp.sum(jnp.where(block_ids == source, task_ids, 0))
        product = inner_rows(own_block, visiting)
        piece = jnp.where(own_task == source_task, product * factor, jnp.float32(0.0))
        starts = (jnp.int32(0), source, jnp.int32(0))
        return lax.dynamic_update_slice(result, piece[:, None, :], starts)

    result = jnp.zeros((block_rows, groups, share_rows), jnp.float32)
    result = place(result, mine, group_index)

    def advance(offset, carried):
        visiting, result = carried
        visiting = from_behind(visiting, "dp", 1)
        source = (group_index - offset) % groups
        return (visiting, place(result, visiting, source))

    _, result = lax.fori_loop(1, groups, advance, (mine, result))
    return result


def solution(mesh):
    in_specs = (
        P("dp", None, "tensor"),
        P("dp", None, "tensor"),
        P("tensor", None),
        P("tensor", None),
        P("dp"),
        P(),
    )
    out_specs = P("dp", None, "tensor")
    return jax.shard_map(body, mesh=mesh, in_specs=in_specs, out_specs=out_specs, check_vma=False)
```

profile of v0, /device:TPU:128, one launch (start us, length us, event | category | flops | bytes accessed | tf_op | source)
XLA Modules:
  0.0 518.5 jit_solution(16584083541157340473)
XLA Ops:
  8.9 3.3 fusion.13
  14.5 292.5 %all-reduce.2.cloned.1.call-done = f32[64,32,128]{2,1,0:T(8,128)} async-done(((f32[64,32,128]{2,1,0:T(8,128)}), f32[64,32,128]{2,1,0:T(8,128)}) %all-reduce.2.cloned.1.call-update) | async-done | bytes 1048592 | tf_op jit(solution)/shard_map/psum | solution.py:57
  307.0 6.2 %multiply_reduce_fusion = (f32[64]{0:T(128)S(1)}, f32[64,64,64]{2,1,0:T(8,128)S(1)}) fusion(f32[64,32,128]{2,1,0:T(8,128)} %all-reduce.2.cloned.1.call-done, f32[64,32]{1,0:T(8,128)S(1)} %fusion.11), kind=kOutput, calls=%fused_computation.7 | convolution fusion | flops 101318592 | bytes 3154176 | tf_op jit(solution)/shard_map/slk,slm->skm/dot_general | solution.py:23
  317.2 193.9 %while.18 = (s32[]{:T(128)}, f32[2,4096]{1,0:T(2,128)S(1)}, f32[64,16,2]{0,2,1:T(2,128)S(1)}, s32[]{:T(128)}, s32[16]{0:T(128)S(1)}, /*index=5*/s32[]{:T(128)}, ...) while((s32[]{:T(128)}, f32[2,4096]{1,0:T(2,128)S(1)}, ...), condition=%wide.region_5.6_spmd.clone, body=%wide.region_3.0_spmd.clone.sunk | while | flops 6291777 | bytes 1279366 | solution.py:79
  317.2 3.4 collective-permute-start
  322.7 7.5 %collective-permute-done = f32[2,4096]{1,0:T(2,128)S(1)} collective-permute-done((f32[2,4096]{1,0:T(2,128)S(1)}, f32[2,4096]{1,0:T(2,128)S(1)}, u32[]{:S(2)}, u32[]{:S(2)}) %collective-permute-start) | collective-permute-done | bytes 32800 | tf_op jit(solution)/shard_map/while/body/eval_jaxpr/ppermute | solution.py:12
  331.1 1.9 collective-permute-start
  335.1 8.0 %collective-permute-done = f32[2,4096]{1,0:T(2,128)S(1)} collective-permute-done((f32[2,4096]{1,0:T(2,128)S(1)}, f32[2,4096]{1,0:T(2,128)S(1)}, u32[]{:S(2)}, u32[]{:S(2)}) %collective-permute-start) | collective-permute-done | bytes 32800 | tf_op jit(solution)/shard_map/while/body/eval_jaxpr/ppermute | solution.py:12
  344.0 1.9 collective-permute-start
  348.0 8.0 %collective-permute-done = f32[2,4096]{1,0:T(2,128)S(1)} collective-permute-done((f32[2,4096]{1,0:T(2,128)S(1)}, f32[2,4096]{1,0:T(2,128)S(1)}, u32[]{:S(2)}, u32[]{:S(2)}) %collective-permute-start) | collective-permute-done | bytes 32800 | tf_op jit(solution)/shard_map/while/body/eval_jaxpr/ppermute | solution.py:12
  356.9 1.9 collective-permute-start
  360.9 8.3 %collective-permute-done = f32[2,4096]{1,0:T(2,128)S(1)} collective-permute-done((f32[2,4096]{1,0:T(2,128)S(1)}, f32[2,4096]{1,0:T(2,128)S(1)}, u32[]{:S(2)}, u32[]{:S(2)}) %collective-permute-start) | collective-permute-done | bytes 32800 | tf_op jit(solution)/shard_map/while/body/eval_jaxpr/ppermute | solution.py:12
  370.1 1.9 collective-permute-start
  374.1 7.9 %collective-permute-done = f32[2,4096]{1,0:T(2,128)S(1)} collective-permute-done((f32[2,4096]{1,0:T(2,128)S(1)}, f32[2,4096]{1,0:T(2,128)S(1)}, u32[]{:S(2)}, u32[]{:S(2)}) %collective-permute-start) | collective-permute-done | bytes 32800 | tf_op jit(solution)/shard_map/while/body/eval_jaxpr/ppermute | solution.py:12
  386.9 7.9 %collective-permute-done = f32[2,4096]{1,0:T(2,128)S(1)} collective-permute-done((f32[2,4096]{1,0:T(2,128)S(1)}, f32[2,4096]{1,0:T(2,128)S(1)}, u32[]{:S(2)}, u32[]{:S(2)}) %collective-permute-start) | collective-permute-done | bytes 32800 | tf_op jit(solution)/shard_map/while/body/eval_jaxpr/ppermute | solution.py:12
  399.6 8.3 %collective-permute-done = f32[2,4096]{1,0:T(2,128)S(1)} collective-permute-done((f32[2,4096]{1,0:T(2,128)S(1)}, f32[2,4096]{1,0:T(2,128)S(1)}, u32[]{:S(2)}, u32[]{:S(2)}) %collective-permute-start) | collective-permute-done | bytes 32800 | tf_op jit(solution)/shard_map/while/body/eval_jaxpr/ppermute | solution.py:12
  412.8 8.0 %collective-permute-done = f32[2,4096]{1,0:T(2,128)S(1)} collective-permute-done((f32[2,4096]{1,0:T(2,128)S(1)}, f32[2,4096]{1,0:T(2,128)S(1)}, u32[]{:S(2)}, u32[]{:S(2)}) %collective-permute-start) | collective-permute-done | bytes 32800 | tf_op jit(solution)/shard_map/while/body/eval_jaxpr/ppermute | solution.py:12
  425.6 7.9 %collective-permute-done = f32[2,4096]{1,0:T(2,128)S(1)} collective-permute-done((f32[2,4096]{1,0:T(2,128)S(1)}, f32[2,4096]{1,0:T(2,128)S(1)}, u32[]{:S(2)}, u32[]{:S(2)}) %collective-permute-start) | collective-permute-done | bytes 32800 | tf_op jit(solution)/shard_map/while/body/eval_jaxpr/ppermute | solution.py:12
  438.4 8.0 %collective-permute-done = f32[2,4096]{1,0:T(2,128)S(1)} collective-permute-done((f32[2,4096]{1,0:T(2,128)S(1)}, f32[2,4096]{1,0:T(2,128)S(1)}, u32[]{:S(2)}, u32[]{:S(2)}) %collective-permute-start) | collective-permute-done | bytes 32800 | tf_op jit(solution)/shard_map/while/body/eval_jaxpr/ppermute | solution.py:12
  451.3 7.9 %collective-permute-done = f32[2,4096]{1,0:T(2,128)S(1)} collective-permute-done((f32[2,4096]{1,0:T(2,128)S(1)}, f32[2,4096]{1,0:T(2,128)S(1)}, u32[]{:S(2)}, u32[]{:S(2)}) %collective-permute-start) | collective-permute-done | bytes 32800 | tf_op jit(solution)/shard_map/while/body/eval_jaxpr/ppermute | solution.py:12
  464.0 7.9 %collective-permute-done = f32[2,4096]{1,0:T(2,128)S(1)} collective-permute-done((f32[2,4096]{1,0:T(2,128)S(1)}, f32[2,4096]{1,0:T(2,128)S(1)}, u32[]{:S(2)}, u32[]{:S(2)}) %collective-permute-start) | collective-permute-done | bytes 32800 | tf_op jit(solution)/shard_map/while/body/eval_jaxpr/ppermute | solution.py:12
  476.8 7.9 %collective-permute-done = f32[2,4096]{1,0:T(2,128)S(1)} collective-permute-done((f32[2,4096]{1,0:T(2,128)S(1)}, f32[2,4096]{1,0:T(2,128)S(1)}, u32[]{:S(2)}, u32[]{:S(2)}) %collective-permute-start) | collective-permute-done | bytes 32800 | tf_op jit(solution)/shard_map/while/body/eval_jaxpr/ppermute | solution.py:12
  489.5 7.9 %collective-permute-done = f32[2,4096]{1,0:T(2,128)S(1)} collective-permute-done((f32[2,4096]{1,0:T(2,128)S(1)}, f32[2,4096]{1,0:T(2,128)S(1)}, u32[]{:S(2)}, u32[]{:S(2)}) %collective-permute-start) | collective-permute-done | bytes 32800 | tf_op jit(solution)/shard_map/while/body/eval_jaxpr/ppermute | solution.py:12
  502.3 7.9 %collective-permute-done = f32[2,4096]{1,0:T(2,128)S(1)} collective-permute-done((f32[2,4096]{1,0:T(2,128)S(1)}, f32[2,4096]{1,0:T(2,128)S(1)}, u32[]{:S(2)}, u32[]{:S(2)}) %collective-permute-start) | collective-permute-done | bytes 32800 | tf_op jit(solution)/shard_map/while/body/eval_jaxpr/ppermute | solution.py:12
  (76 shorter events, 53.1 us)
Async XLA Ops:
  6.5 1.2 copy-start
  6.5 300.5 %all-reduce.2.cloned.1.call-start = ((), (), s32[]{:S(2)}) async-start(), calls=%async_computation | async-start | bytes 2097152 | tf_op jit(solution)/shard_map/psum | solution.py:57
  12.2 1.5 copy-start.3
  12.2 2.2 copy-start.2
  317.2 13.0 %collective-permute-start = (f32[2,4096]{1,0:T(2,128)S(1)}, f32[2,4096]{1,0:T(2,128)S(1)}, u32[]{:S(2)}, u32[]{:S(2)}) collective-permute-start(f32[2,4096]{1,0:T(2,128)S(1)} %get-tuple-element.292), channel_id=1, source_target_pairs={{0,32},{32,64},{64,96},{96,128},{128,160},{160,192},{192,224},{224... | collective-permute-start | bytes 98312 | tf_op jit(solution)/shard_map/while/body/eval_jaxpr/ppermute | solution.py:12
  331.1 12.0 %collective-permute-start = (f32[2,4096]{1,0:T(2,128)S(1)}, f32[2,4096]{1,0:T(2,128)S(1)}, u32[]{:S(2)}, u32[]{:S(2)}) collective-permute-start(f32[2,4096]{1,0:T(2,128)S(1)} %get-tuple-element.292), channel_id=1, source_target_pairs={{0,32},{32,64},{64,96},{96,128},{128,160},{160,192},{192,224},{224... | collective-permute-start | bytes 98312 | tf_op jit(solution)/shard_map/while/body/eval_jaxpr/ppermute | solution.py:12
  344.0 12.0 %collective-permute-start = (f32[2,4096]{1,0:T(2,128)S(1)}, f32[2,4096]{1,0:T(2,128)S(1)}, u32[]{:S(2)}, u32[]{:S(2)}) collective-permute-start(f32[2,4096]{1,0:T(2,128)S(1)} %get-tuple-element.292), channel_id=1, source_target_pairs={{0,32},{32,64},{64,96},{96,128},{128,160},{160,192},{192,224},{224... | collective-permute-start | bytes 98312 | tf_op jit(solution)/shard_map/while/body/eval_jaxpr/ppermute | solution.py:12
  356.9 12.2 %collective-permute-start = (f32[2,4096]{1,0:T(2,128)S(1)}, f32[2,4096]{1,0:T(2,128)S(1)}, u32[]{:S(2)}, u32[]{:S(2)}) collective-permute-start(f32[2,4096]{1,0:T(2,128)S(1)} %get-tuple-element.292), channel_id=1, source_target_pairs={{0,32},{32,64},{64,96},{96,128},{128,160},{160,192},{192,224},{224... | collective-permute-start | bytes 98312 | tf_op jit(solution)/shard_map/while/body/eval_jaxpr/ppermute | solution.py:12
  370.1 11.9 %collective-permute-start = (f32[2,4096]{1,0:T(2,128)S(1)}, f32[2,4096]{1,0:T(2,128)S(1)}, u32[]{:S(2)}, u32[]{:S(2)}) collective-permute-start(f32[2,4096]{1,0:T(2,128)S(1)} %get-tuple-element.292), channel_id=1, source_target_pairs={{0,32},{32,64},{64,96},{96,128},{128,160},{160,192},{192,224},{224... | collective-permute-start | bytes 98312 | tf_op jit(solution)/shard_map/while/body/eval_jaxpr/ppermute | solution.py:12
  382.9 11.8 %collective-permute-start = (f32[2,4096]{1,0:T(2,128)S(1)}, f32[2,4096]{1,0:T(2,128)S(1)}, u32[]{:S(2)}, u32[]{:S(2)}) collective-permute-start(f32[2,4096]{1,0:T(2,128)S(1)} %get-tuple-element.292), channel_id=1, source_target_pairs={{0,32},{32,64},{64,96},{96,128},{128,160},{160,192},{192,224},{224... | collective-permute-start | bytes 98312 | tf_op jit(solution)/shard_map/while/body/eval_jaxpr/ppermute | solution.py:12
  395.6 12.2 %collective-permute-start = (f32[2,4096]{1,0:T(2,128)S(1)}, f32[2,4096]{1,0:T(2,128)S(1)}, u32[]{:S(2)}, u32[]{:S(2)}) collective-permute-start(f32[2,4096]{1,0:T(2,128)S(1)} %get-tuple-element.292), channel_id=1, source_target_pairs={{0,32},{32,64},{64,96},{96,128},{128,160},{160,192},{192,224},{224... | collective-permute-start | bytes 98312 | tf_op jit(solution)/shard_map/while/body/eval_jaxpr/ppermute | solution.py:12
  408.8 11.9 %collective-permute-start = (f32[2,4096]{1,0:T(2,128)S(1)}, f32[2,4096]{1,0:T(2,128)S(1)}, u32[]{:S(2)}, u32[]{:S(2)}) collective-permute-start(f32[2,4096]{1,0:T(2,128)S(1)} %get-tuple-element.292), channel_id=1, source_target_pairs={{0,32},{32,64},{64,96},{96,128},{128,160},{160,192},{192,224},{224... | collective-permute-start | bytes 98312 | tf_op jit(solution)/shard_map/while/body/eval_jaxpr/ppermute | solution.py:12
  421.7 11.9 %collective-permute-start = (f32[2,4096]{1,0:T(2,128)S(1)}, f32[2,4096]{1,0:T(2,128)S(1)}, u32[]{:S(2)}, u32[]{:S(2)}) collective-permute-start(f32[2,4096]{1,0:T(2,128)S(1)} %get-tuple-element.292), channel_id=1, source_target_pairs={{0,32},{32,64},{64,96},{96,128},{128,160},{160,192},{192,224},{224... | collective-permute-start | bytes 98312 | tf_op jit(solution)/shard_map/while/body/eval_jaxpr/ppermute | solution.py:12
  434.4 11.9 %collective-permute-start = (f32[2,4096]{1,0:T(2,128)S(1)}, f32[2,4096]{1,0:T(2,128)S(1)}, u32[]{:S(2)}, u32[]{:S(2)}) collective-permute-start(f32[2,4096]{1,0:T(2,128)S(1)} %get-tuple-element.292), channel_id=1, source_target_pairs={{0,32},{32,64},{64,96},{96,128},{128,160},{160,192},{192,224},{224... | collective-permute-start | bytes 98312 | tf_op jit(solution)/shard_map/while/body/eval_jaxpr/ppermute | solution.py:12
  447.3 11.8 %collective-permute-start = (f32[2,4096]{1,0:T(2,128)S(1)}, f32[2,4096]{1,0:T(2,128)S(1)}, u32[]{:S(2)}, u32[]{:S(2)}) collective-permute-start(f32[2,4096]{1,0:T(2,128)S(1)} %get-tuple-element.292), channel_id=1, source_target_pairs={{0,32},{32,64},{64,96},{96,128},{128,160},{160,192},{192,224},{224... | collective-permute-start | bytes 98312 | tf_op jit(solution)/shard_map/while/body/eval_jaxpr/ppermute | solution.py:12
  460.0 11.8 %collective-permute-start = (f32[2,4096]{1,0:T(2,128)S(1)}, f32[2,4096]{1,0:T(2,128)S(1)}, u32[]{:S(2)}, u32[]{:S(2)}) collective-permute-start(f32[2,4096]{1,0:T(2,128)S(1)} %get-tuple-element.292), channel_id=1, source_target_pairs={{0,32},{32,64},{64,96},{96,128},{128,160},{160,192},{192,224},{224... | collective-permute-start | bytes 98312 | tf_op jit(solution)/shard_map/while/body/eval_jaxpr/ppermute | solution.py:12
  472.8 11.8 %collective-permute-start = (f32[2,4096]{1,0:T(2,128)S(1)}, f32[2,4096]{1,0:T(2,128)S(1)}, u32[]{:S(2)}, u32[]{:S(2)}) collective-permute-start(f32[2,4096]{1,0:T(2,128)S(1)} %get-tuple-element.292), channel_id=1, source_target_pairs={{0,32},{32,64},{64,96},{96,128},{128,160},{160,192},{192,224},{224... | collective-permute-start | bytes 98312 | tf_op jit(solution)/shard_map/while/body/eval_jaxpr/ppermute | solution.py:12
  485.6 11.8 %collective-permute-start = (f32[2,4096]{1,0:T(2,128)S(1)}, f32[2,4096]{1,0:T(2,128)S(1)}, u32[]{:S(2)}, u32[]{:S(2)}) collective-permute-start(f32[2,4096]{1,0:T(2,128)S(1)} %get-tuple-element.292), channel_id=1, source_target_pairs={{0,32},{32,64},{64,96},{96,128},{128,160},{160,192},{192,224},{224... | collective-permute-start | bytes 98312 | tf_op jit(solution)/shard_map/while/body/eval_jaxpr/ppermute | solution.py:12
  498.3 11.8 %collective-permute-start = (f32[2,4096]{1,0:T(2,128)S(1)}, f32[2,4096]{1,0:T(2,128)S(1)}, u32[]{:S(2)}, u32[]{:S(2)}) collective-permute-start(f32[2,4096]{1,0:T(2,128)S(1)} %get-tuple-element.292), channel_id=1, source_target_pairs={{0,32},{32,64},{64,96},{96,128},{128,160},{160,192},{192,224},{224... | collective-permute-start | bytes 98312 | tf_op jit(solution)/shard_map/while/body/eval_jaxpr/ppermute | solution.py:12
  511.1 0.6 copy-start.1
Sparse Core Ops, SparseCore 0:
  13.9 293.0 all-reduce.1
where the time goes:
time: 519 us
  waiting for transfers between devices  411 us (79%)
  starting transfers between devices  30.3 us (6%)
  matrix products  25.5 us (5%)
  loops' own time  20 us (4%)
  between operations  13.5 us (3%)
  other arithmetic  12.9 us (2%)
    psum x1, waiting for transfers between devices, body(): summed = lax.psum(partial_value, 'tensor')  292 us
    ppermute x15, waiting for transfers between devices, from_behind(): return lax.ppermute(value, axis, pairs)  119 us
    ppermute x15, starting transfers between devices, from_behind(): return lax.ppermute(value, axis, pairs)  30.3 us
    another operation x1, loops' own time, body(): _, result = lax.fori_loop(1, groups, advance, (mine, result))  20 us
    dot_general x16, matrix products, inner_rows(): lax.dot_general(left, right, (((1,), (1,)), ((), ())), preferred_element_...  14.8 us
    reduce_sum x15, other arithmetic, place(): source_task = jnp.sum(jnp.where(block_ids == source, task_ids, 0))  10.7 us
  transfers between devices with their start and end apart: 16, of which 16 were waited for; matrix products, arithmetic and copies ran while one was open for 2% of the time, Pallas kernels for 0%

commit v1 on v0

v1 whole, which is shorter than its diff:
```python
import jax
import jax.numpy as jnp
import numpy as np
from jax import lax
from jax.experimental import pallas as pl
from jax.experimental.pallas import tpu as pltpu
from jax.sharding import Mesh
from jax.sharding import PartitionSpec as P

epsilon = 1e-06

AXES = ("z_hi", "y", "z_lo", "x", "core")
SIZES = (4, 4, 4, 4, 2)
DP = ("z_hi", "y")
TENSOR = ("z_lo", "x", "core")
CHIPS = ("z_lo", "x")
ROW = ("x", "core")

HIGHEST = lax.Precision.HIGHEST
VMEM = pl.BlockSpec(memory_space=pltpu.VMEM)
SMEM = pl.BlockSpec(memory_space=pltpu.SMEM)
PROJECT_VMEM = 62 * 1024 * 1024
SMALL = pltpu.CompilerParams(vmem_limit_bytes=8 * 1024 * 1024)


def contract(left, right, dims):
    return lax.dot_general(
        left, right, (dims, ((), ())), preferred_element_type=jnp.float32, precision=HIGHEST
    )


def exchange(value, axes):
    return lax.all_to_all(value, axes, 0, 0, tiled=True)


def gather(value, axis):
    copies = jnp.broadcast_to(value[None], (lax.axis_size(axis),) + value.shape)
    return exchange(copies, axis)


def project_kernel(core_ref, hidden_ref, grad_ref, in_ref, out_ref, terms_ref):
    pairs, rows, _ = hidden_ref.shape
    rank = in_ref.shape[0]
    dims = (((1,), (1,)), ((), ()))
    hidden = hidden_ref[...].reshape(pairs * rows, -1)
    grad = grad_ref[...].reshape(pairs * rows, -1)
    left = lax.dot_general(hidden, in_ref[...], dims, preferred_element_type=jnp.float32)
    right = lax.dot_general(grad, out_ref[...], dims, preferred_element_type=jnp.float32)
    terms_ref[...] = jnp.concatenate([left, right], axis=1).reshape(pairs, rows, 2 * rank)


def project(core, hidden, grad, weights_in, weights_out, steps):
    pairs, cores, rows, wide = hidden.shape
    narrow = grad.shape[3]
    rank = weights_in.shape[0]
    block = pairs // steps
    return pl.pallas_call(
        project_kernel,
        grid_spec=pltpu.PrefetchScalarGridSpec(
            num_scalar_prefetch=1,
            grid=(steps,),
            in_specs=[
                pl.BlockSpec((block, None, rows, wide), lambda i, c: (i, c[0], 0, 0)),
                pl.BlockSpec((block, None, rows, narrow), lambda i, c: (i, c[0], 0, 0)),
                pl.BlockSpec((rank, wide), lambda i, c: (0, 0)),
                pl.BlockSpec((rank, narrow), lambda i, c: (0, 0)),
            ],
            out_specs=pl.BlockSpec((block, rows, 2 * rank), lambda i, c: (i, 0, 0)),
        ),
        out_shape=jax.ShapeDtypeStruct((pairs, rows, 2 * rank), jnp.float32),
        compiler_params=pltpu.CompilerParams(vmem_limit_bytes=PROJECT_VMEM),
        cost_estimate=pl.CostEstimate(
            flops=2 * pairs * rows * rank * (wide + narrow),
            bytes_accessed=2 * pairs * rows * (wide + narrow) + 8 * pairs * rows * rank,
            transcendentals=0,
        ),
        name="project",
    )(core, hidden, grad, weights_in, weights_out)


def sketch_kernel(place_ref, lengths_ref, terms_ref, out_ref):
    first = place_ref[0]
    total = jnp.sum(terms_ref[...], axis=0)
    share = out_ref.shape[1] // 2
    seq_len, rank = total.shape[0] // 2, total.shape[1] // 2
    slot = lax.broadcasted_iota(jnp.int32, (seq_len, rank), 0)
    for s in range(2):
        mine = total[s * seq_len : (s + 1) * seq_len]
        live = (slot < lengths_ref[first + s]).astype(jnp.float32)
        sketch = contract(mine[:, :rank] * live, mine[:, rank:], ((0,), (0,)))
        mean = jnp.sum(sketch * sketch) / (rank * rank)
        unit = sketch / jnp.sqrt(jnp.full((1, 1), mean, jnp.float32) + epsilon)
        wide = jnp.concatenate([unit[: rank // 2], unit[rank // 2 :]], axis=1)
        for j in range(out_ref.shape[0]):
            out_ref[j, s * share : (s + 1) * share, :] = wide[j * share : (j + 1) * share]


def sketches(place, lengths, terms, parts):
    rows = terms.shape[1] // (2 * parts)
    return pl.pallas_call(
        sketch_kernel,
        in_specs=[SMEM, SMEM, VMEM],
        out_specs=VMEM,
        out_shape=jax.ShapeDtypeStruct((parts, 2 * rows, terms.shape[2]), jnp.float32),
        compiler_params=SMALL,
        name="sketches",
    )(place, lengths, terms)


def gram_kernel(rows_ref, cols_ref, out_ref, held):
    share = 4
    parts, blocks, lanes = out_ref.shape
    n_rows = rows_ref.shape[0] // share
    n_cols = cols_ref.shape[0] // (2 * share)
    halves = [jnp.zeros((n_cols, n_rows), jnp.float32) for _ in range(2)]
    for r in range(share):
        right = rows_ref[pl.ds(r, n_rows, stride=share), :]
        for s in range(2):
            left = cols_ref[pl.ds(s * share + r, n_cols, stride=2 * share), :]
            halves[s] = halves[s] + contract(left, right, ((1,), (1,)))
    held[...] = jnp.concatenate(halves, axis=1)
    for d in range(parts):
        out_ref[d] = held[pl.ds(d, blocks, stride=parts), :]


def gram(rows, cols, parts, blocks):
    lanes = 2 * (rows.shape[0] // 4)
    return pl.pallas_call(
        gram_kernel,
        in_specs=[VMEM, VMEM],
        out_specs=VMEM,
        out_shape=jax.ShapeDtypeStruct((parts, blocks, lanes), jnp.float32),
        scratch_shapes=[pltpu.VMEM((parts * blocks, lanes), jnp.float32)],
        compiler_params=SMALL,
        name="gram",
    )(rows, cols)


def finish_kernel(place_ref, tasks_ref, terms_ref, out_ref):
    group = place_ref[0]
    z_own = place_ref[1]
    n_y, n_z, seqs = 4, 4, out_ref.shape[2]
    total = jnp.sum(terms_ref[...], axis=0) * (1.0 / seqs)
    for y in range(n_y):
        for k in range(n_z):
            z = (z_own + n_z - k) % n_z
            block = z * n_y + y
            same = tasks_ref[block] == tasks_ref[group]
            row = total[y * n_z + k : y * n_z + k + 1]
            row = jnp.where(same, row, jnp.float32(0.0))
            out_ref[block] = jnp.concatenate([row[:, :seqs], row[:, seqs:]], axis=0)


def finish(place, tasks, terms):
    _, groups, lanes = terms.shape
    return pl.pallas_call(
        finish_kernel,
        in_specs=[SMEM, SMEM, VMEM],
        out_specs=VMEM,
        out_shape=jax.ShapeDtypeStruct((groups, 2, lanes // 2), jnp.float32),
        compiler_params=SMALL,
        name="finish",
    )(place, tasks, terms)


def body(hidden, out_grad, proj_in, proj_out, lengths, task_ids):
    block_rows, seq_len, _ = hidden.shape
    rank = proj_in.shape[1]
    groups = lax.axis_size(DP)
    parts = lax.axis_size(ROW)
    chips = lax.axis_size(CHIPS)
    share = block_rows // lax.axis_size(TENSOR)
    pair_rows = share * seq_len
    core = lax.axis_index("core")
    slice_index = lax.axis_index(TENSOR)
    group_index = lax.axis_index(DP)

    hidden = hidden.reshape(chips, 2, pair_rows, -1)
    out_grad = out_grad.reshape(chips, 2, pair_rows, -1)
    own = jnp.reshape(core, (1,)).astype(jnp.int32)
    weights = (proj_in.T, proj_out.T)
    send = project(1 - own, hidden, out_grad, *weights, 2)
    keep = project(own, hidden, out_grad, *weights, 2)
    mine = keep + lax.ppermute(send, "core", [(0, 1), (1, 0)])
    terms = exchange(mine, CHIPS)
    place = jnp.reshape(slice_index * share, (1,)).astype(jnp.int32)
    units = sketches(place, lengths, terms, parts)
    entries = exchange(units, ROW).reshape(-1, 2 * rank)
    n_z = lax.axis_size("z_hi")
    far = [entries]
    for k in range(1, n_z):
        far.append(lax.ppermute(entries, "z_hi", [(i, (i + k) % n_z) for i in range(n_z)]))
    rows = gather(entries, "z_lo").reshape(-1, 2 * rank)
    cols = gather(jnp.stack(far), "y").reshape(-1, 2 * rank)
    partial_value = gram(rows, cols, parts, groups)
    place = jnp.stack([group_index, lax.axis_index("z_hi")]).astype(jnp.int32)
    return finish(place, task_ids, exchange(partial_value, ROW)).transpose(2, 0, 1)


def solution(mesh):
    fine = Mesh(np.asarray(mesh.devices).reshape(SIZES), AXES)
    in_specs = (
        P(DP, None, TENSOR),
        P(DP, None, TENSOR),
        P(TENSOR, None),
        P(TENSOR, None),
        P(DP),
        P(),
    )
    out_specs = P(DP, None, TENSOR)
    return jax.shard_map(body, mesh=fine, in_specs=in_specs, out_specs=out_specs, check_vma=False)
```

time: 519 us -> 102 us (0.20)
  the two profiles are of different devices: /device:TPU:128 before, /device:TPU:1 now
where the time goes in v1:
time: 102 us; the launch traced here: 101 us
  starting transfers between devices  48.6 us (48%)
  waiting for transfers between devices  30.5 us (30%)
  Pallas kernels  9.71 us (10%)
  blocking collectives  8.96 us (9%)
  other arithmetic  2.02 us (2%)
  local copies, waits for them, and re-layouts  1.52 us (1%)
    all_to_all x4, waiting for transfers between devices, exchange(): return lax.all_to_all(value, axes, 0, 0, tiled=True)  26.5 us
    ppermute x3, starting transfers between devices, body(): lax.ppermute(entries, 'z_hi', [(i, (i + k) % n_z) for i in range(n_z)])  21.5 us
    all_to_all x4, starting transfers between devices, exchange(): return lax.all_to_all(value, axes, 0, 0, tiled=True)  18.3 us
    all_to_all x1, blocking collectives, exchange(): return lax.all_to_all(value, axes, 0, 0, tiled=True)  8.96 us
    ppermute x1, starting transfers between devices, body(): mine = keep + lax.ppermute(send, 'core', [(0, 1), (1, 0)])  8.85 us
    pallas_call x2, Pallas kernels, project(): pl.pallas_call(project_kernel, grid_spec=pltpu.PrefetchScalarGridSpec(num...  6.12 us
    ppermute x3, waiting for transfers between devices, body(): lax.ppermute(entries, 'z_hi', [(i, (i + k) % n_z) for i in range(n_z)])  4.03 us
  transfers between devices with their start and end apart: 8, of which 5 were waited for; matrix products, arithmetic and copies ran while one was open for 0% of the time, Pallas kernels for 3%

profile of v1, /device:TPU:1, one launch (start us, length us, event | category | flops | bytes accessed | tf_op | source)
XLA Modules:
  0.0 101.5 jit_solution(11911043569777114535)
XLA Ops:
  0.0 3.0 %project.3 = f32[16,64,128]{2,1,0:T(8,128)} custom-call(s32[1]{0:T(128)S(6)} %sub.3.core_ref, bf16[16,2,64,896]{3,2,1,0:T(8,128)(2,1)} %bitcast.18, bf16[16,2,64,256]{3,2,1,0:T(8,128)(2,1)} %bitcast.20, bf16[64,896]{1,0:T(8,128)(2,1)} %bitcast.22, bf16[64,256]{1,0:T(8,128)(2,1)} %bitcast.29), custom_call_target="tpu_custom_call" | custom-call | flops 150994944 | bytes 2883584 | tf_op jit(solution)/shard_map/project/pallas_call | solution.py:57
  3.1 8.9 %collective-permute-start = (f32[16,64,128]{2,1,0:T(8,128)}, f32[16,64,128]{2,1,0:T(8,128)S(1)}, u32[]{:S(2)}, u32[]{:S(2)}) collective-permute-start(f32[16,64,128]{2,1,0:T(8,128)} %project.3), channel_id=1, source_target_pairs={{0,1},{1,0},{2,3},{3,2},{4,5},{5,4},{6,7},{7,6},{8,9},{9,8},{10,11... | collective-permute-start | bytes 1572872 | tf_op jit(solution)/shard_map/ppermute | solution.py:184
  11.9 3.1 %project.2 = f32[16,64,128]{2,1,0:T(8,128)} custom-call(s32[1]{0:T(128)} %bitcast.3.core_ref, bf16[16,2,64,896]{3,2,1,0:T(8,128)(2,1)} %bitcast.19, bf16[16,2,64,256]{3,2,1,0:T(8,128)(2,1)} %bitcast.21, bf16[64,896]{1,0:T(8,128)(2,1)} %bitcast.23, bf16[64,256]{1,0:T(8,128)(2,1)} %bitcast.30), custom_call_target="tpu_custom_call" | custom-call | flops 150994944 | bytes 2883584 | tf_op jit(solution)/shard_map/project/pallas_call | solution.py:57
  15.0 0.0 collective-permute-done
  15.0 1.9 %add.15 = f32[16,64,128]{2,1,0:T(8,128)} add(f32[16,64,128]{2,1,0:T(8,128)} %project.2, f32[16,64,128]{2,1,0:T(8,128)S(1)} %collective-permute-done) | non-fusion elementwise | flops 131072 | bytes 1572864 | tf_op jit(solution)/shard_map/add | solution.py:184
  16.9 3.6 %all-to-all-start = ((f32[16,64,128]{2,1,0:T(8,128)}), f32[16,64,128]{2,1,0:T(8,128)S(1)}, u32[]{:S(2)}, u32[]{:S(2)}) async-start(f32[16,64,128]{2,1,0:T(8,128)} %add.15), calls=%async_computation | async-start | bytes 1048576 | tf_op jit(solution)/shard_map/all_to_all | solution.py:33
  20.5 14.8 %all-to-all-done.terms_ref = f32[16,64,128]{2,1,0:T(8,128)S(1)} async-done(((f32[16,64,128]{2,1,0:T(8,128)}), f32[16,64,128]{2,1,0:T(8,128)S(1)}, u32[]{:S(2)}, u32[]{:S(2)}) %all-to-all-start) | async-done | bytes 524320 | tf_op jit(solution)/shard_map/all_to_all | solution.py:33
  35.3 1.0 %sketches.1 = f32[8,8,128]{2,1,0:T(8,128)S(1)} custom-call(s32[1]{0:T(128)} %bitcast.2.place_ref, s32[64]{0:T(128)S(1)} %copy-done.1, f32[16,64,128]{2,1,0:T(8,128)S(1)} %all-to-all-done.terms_ref), custom_call_target="tpu_custom_call" | custom-call | tf_op jit(solution)/shard_map/sketches/pallas_call | solution.py:100
  36.3 9.0 %all_to_all.25 = f32[8,8,128]{2,1,0:T(8,128)S(1)} all-to-all(f32[8,8,128]{2,1,0:T(8,128)S(1)} %sketches.1), channel_id=1, replica_groups=mesh['z_hi'=4,'y'=4,'z_lo'=4,'x'=4,'core'=2] {'x','core'}, dimensions={0} | all-to-all | bytes 65536 | tf_op jit(solution)/shard_map/all_to_all | solution.py:33
  45.3 0.7 broadcast_in_dim.14
  45.9 3.3 %all-to-all-start.2 = ((f32[4,64,128]{2,1,0:T(8,128)}), f32[4,64,128]{2,1,0:T(8,128)S(1)}, u32[]{:S(2)}, u32[]{:S(2)}) async-start(f32[4,64,128]{2,1,0:T(8,128)} %broadcast_in_dim.14), calls=%async_computation.2 | async-start | bytes 262144 | tf_op jit(solution)/shard_map/all_to_all | solution.py:33
  49.3 8.4 %collective-permute-start.1 = (f32[64,128]{1,0:T(8,128)S(1)}, f32[64,128]{1,0:T(8,128)S(1)}, u32[]{:S(2)}, u32[]{:S(2)}) collective-permute-start(f32[64,128]{1,0:T(8,128)S(1)} %bitcast.25), channel_id=1, source_target_pairs={{0,128},{128,256},{256,384},{384,0},{1,129},{129,257},{257,385},{3... | collective-permute-start | bytes 98312 | tf_op jit(solution)/shard_map/ppermute | solution.py:192
  57.6 7.9 %collective-permute-start.2 = (f32[64,128]{1,0:T(8,128)S(1)}, f32[64,128]{1,0:T(8,128)S(1)}, u32[]{:S(2)}, u32[]{:S(2)}) collective-permute-start(f32[64,128]{1,0:T(8,128)S(1)} %bitcast.26), channel_id=1, source_target_pairs={{0,256},{128,384},{256,0},{384,128},{1,257},{129,385},{257,1},{385... | collective-permute-start | bytes 98312 | tf_op jit(solution)/shard_map/ppermute | solution.py:192
  65.6 5.2 %collective-permute-start.3 = (f32[64,128]{1,0:T(8,128)S(1)}, f32[64,128]{1,0:T(8,128)S(1)}, u32[]{:S(2)}, u32[]{:S(2)}) collective-permute-start(f32[64,128]{1,0:T(8,128)S(1)} %bitcast.27), channel_id=1, source_target_pairs={{0,384},{128,0},{256,128},{384,256},{1,385},{129,1},{257,129},{385... | collective-permute-start | bytes 98312 | tf_op jit(solution)/shard_map/ppermute | solution.py:192
  70.8 0.3 collective-permute-done.2
  71.0 3.8 %collective-permute-done.3 = f32[64,128]{1,0:T(8,128)S(1)} collective-permute-done((f32[64,128]{1,0:T(8,128)S(1)}, f32[64,128]{1,0:T(8,128)S(1)}, u32[]{:S(2)}, u32[]{:S(2)}) %collective-permute-start.3) | collective-permute-done | bytes 32800 | tf_op jit(solution)/shard_map/ppermute | solution.py:192
  74.8 0.9 broadcast_in_dim.15
  75.7 4.2 %all-to-all-start.3 = ((f32[4,4,64,128]{3,2,1,0:T(8,128)}), f32[4,4,64,128]{3,2,1,0:T(8,128)S(1)}, u32[]{:S(2)}, u32[]{:S(2)}) async-start(f32[4,4,64,128]{3,2,1,0:T(8,128)} %broadcast_in_dim.15), calls=%async_computation.3 | async-start | bytes 1048576 | tf_op jit(solution)/shard_map/all_to_all | solution.py:33
  79.9 6.9 %all-to-all-done.3 = f32[4,4,64,128]{3,2,1,0:T(8,128)S(1)} async-done(((f32[4,4,64,128]{3,2,1,0:T(8,128)}), f32[4,4,64,128]{3,2,1,0:T(8,128)S(1)}, u32[]{:S(2)}, u32[]{:S(2)}) %all-to-all-start.3) | async-done | bytes 524320 | tf_op jit(solution)/shard_map/all_to_all | solution.py:33
  86.8 1.3 %gram.1 = f32[8,16,128]{2,1,0:T(8,128)} custom-call(f32[256,128]{1,0:T(8,128)S(1)} %bitcast.17, f32[1024,128]{1,0:T(8,128)S(1)} %bitcast.16), custom_call_target="tpu_custom_call" | custom-call | tf_op jit(solution)/shard_map/gram/pallas_call | solution.py:128
  88.1 7.2 %all-to-all-start.4 = ((f32[8,16,128]{2,1,0:T(8,128)}), f32[8,16,128]{2,1,0:T(8,128)S(1)}, u32[]{:S(2)}, u32[]{:S(2)}) async-start(f32[8,16,128]{2,1,0:T(8,128)} %gram.1), calls=%async_computation.4 | async-start | bytes 131072 | tf_op jit(solution)/shard_map/all_to_all | solution.py:33
  95.3 0.1 pad_add_fusion.place_ref
  95.4 4.8 %all-to-all-done.4.terms_ref = f32[8,16,128]{2,1,0:T(8,128)S(1)} async-done(((f32[8,16,128]{2,1,0:T(8,128)}), f32[8,16,128]{2,1,0:T(8,128)S(1)}, u32[]{:S(2)}, u32[]{:S(2)}) %all-to-all-start.4) | async-done | bytes 65568 | tf_op jit(solution)/shard_map/all_to_all | solution.py:33
  100.2 1.3 %finish.1 = f32[16,2,64]{2,1,0:T(2,128)} custom-call(s32[2]{0:T(128)S(1)} %pad_add_fusion.place_ref, s32[16]{0:T(128)S(1)} %copy-done, f32[8,16,128]{2,1,0:T(8,128)S(1)} %all-to-all-done.4.terms_ref), custom_call_target="tpu_custom_call" | custom-call | tf_op jit(solution)/shard_map/finish/pallas_call | solution.py:156
  (7 shorter events, 0.0 us)
Async XLA Ops:
  3.0 32.2 %copy-start.1 = (s32[64]{0:T(128)S(1)}, s32[64]{0:T(128)}, u32[]{:S(2)}) copy-start(s32[64]{0:T(128)} %lengths_ref.1) | copy-start | bytes 772
  3.1 11.9 %collective-permute-start = (f32[16,64,128]{2,1,0:T(8,128)}, f32[16,64,128]{2,1,0:T(8,128)S(1)}, u32[]{:S(2)}, u32[]{:S(2)}) collective-permute-start(f32[16,64,128]{2,1,0:T(8,128)} %project.3), channel_id=1, source_target_pairs={{0,1},{1,0},{2,3},{3,2},{4,5},{5,4},{6,7},{7,6},{8,9},{9,8},{10,11... | collective-permute-start | bytes 1572872 | tf_op jit(solution)/shard_map/ppermute | solution.py:184
  15.0 85.2 %copy-start = (s32[16]{0:T(128)S(1)}, s32[16]{0:T(128)}, u32[]{:S(2)}) copy-start(s32[16]{0:T(128)} %tasks_ref.1) | copy-start | bytes 196
  16.9 18.4 %all-to-all-start = ((f32[16,64,128]{2,1,0:T(8,128)}), f32[16,64,128]{2,1,0:T(8,128)S(1)}, u32[]{:S(2)}, u32[]{:S(2)}) async-start(f32[16,64,128]{2,1,0:T(8,128)} %add.15), calls=%async_computation | async-start | bytes 1048576 | tf_op jit(solution)/shard_map/all_to_all | solution.py:33
  45.9 28.9 %all-to-all-start.2 = ((f32[4,64,128]{2,1,0:T(8,128)}), f32[4,64,128]{2,1,0:T(8,128)S(1)}, u32[]{:S(2)}, u32[]{:S(2)}) async-start(f32[4,64,128]{2,1,0:T(8,128)} %broadcast_in_dim.14), calls=%async_computation.2 | async-start | bytes 262144 | tf_op jit(solution)/shard_map/all_to_all | solution.py:33
  49.3 21.5 %collective-permute-start.1 = (f32[64,128]{1,0:T(8,128)S(1)}, f32[64,128]{1,0:T(8,128)S(1)}, u32[]{:S(2)}, u32[]{:S(2)}) collective-permute-start(f32[64,128]{1,0:T(8,128)S(1)} %bitcast.25), channel_id=1, source_target_pairs={{0,128},{128,256},{256,384},{384,0},{1,129},{129,257},{257,385},{3... | collective-permute-start | bytes 98312 | tf_op jit(solution)/shard_map/ppermute | solution.py:192
  57.6 13.4 %collective-permute-start.2 = (f32[64,128]{1,0:T(8,128)S(1)}, f32[64,128]{1,0:T(8,128)S(1)}, u32[]{:S(2)}, u32[]{:S(2)}) collective-permute-start(f32[64,128]{1,0:T(8,128)S(1)} %bitcast.26), channel_id=1, source_target_pairs={{0,256},{128,384},{256,0},{384,128},{1,257},{129,385},{257,1},{385... | collective-permute-start | bytes 98312 | tf_op jit(solution)/shard_map/ppermute | solution.py:192
  65.6 9.2 %collective-permute-start.3 = (f32[64,128]{1,0:T(8,128)S(1)}, f32[64,128]{1,0:T(8,128)S(1)}, u32[]{:S(2)}, u32[]{:S(2)}) collective-permute-start(f32[64,128]{1,0:T(8,128)S(1)} %bitcast.27), channel_id=1, source_target_pairs={{0,384},{128,0},{256,128},{384,256},{1,385},{129,1},{257,129},{385... | collective-permute-start | bytes 98312 | tf_op jit(solution)/shard_map/ppermute | solution.py:192
  75.7 11.1 %all-to-all-start.3 = ((f32[4,4,64,128]{3,2,1,0:T(8,128)}), f32[4,4,64,128]{3,2,1,0:T(8,128)S(1)}, u32[]{:S(2)}, u32[]{:S(2)}) async-start(f32[4,4,64,128]{3,2,1,0:T(8,128)} %broadcast_in_dim.15), calls=%async_computation.3 | async-start | bytes 1048576 | tf_op jit(solution)/shard_map/all_to_all | solution.py:33
  88.1 12.1 %all-to-all-start.4 = ((f32[8,16,128]{2,1,0:T(8,128)}), f32[8,16,128]{2,1,0:T(8,128)S(1)}, u32[]{:S(2)}, u32[]{:S(2)}) async-start(f32[8,16,128]{2,1,0:T(8,128)} %gram.1), calls=%async_computation.4 | async-start | bytes 131072 | tf_op jit(solution)/shard_map/all_to_all | solution.py:33

commit v2 on v1

v2 whole, which is shorter than its diff:
```python
import functools

import jax
import jax.numpy as jnp
import numpy as np
from jax import lax
from jax.experimental import pallas as pl
from jax.experimental.pallas import tpu as pltpu
from jax.sharding import Mesh
from jax.sharding import PartitionSpec as P

epsilon = 1e-06

AXES = ("z_hi", "y", "z_lo", "x", "core")
SIZES = (4, 4, 4, 4, 2)
DP = ("z_hi", "y")
TENSOR = ("z_lo", "x", "core")
CHIPS = ("z_lo", "x")

HIGHEST = lax.Precision.HIGHEST
VMEM = pl.BlockSpec(memory_space=pltpu.VMEM)
SMEM = pl.BlockSpec(memory_space=pltpu.SMEM)
CHUNKS = 4
HBM = pl.BlockSpec(memory_space=pltpu.HBM)
SMALL = pltpu.CompilerParams(vmem_limit_bytes=8 * 1024 * 1024)


def contract(left, right, dims):
    return lax.dot_general(
        left, right, (dims, ((), ())), preferred_element_type=jnp.float32, precision=HIGHEST
    )


def exchange(value, axes):
    return lax.all_to_all(value, axes, 0, 0, tiled=True)


def gather(value, axis):
    copies = jnp.broadcast_to(value[None], (lax.axis_size(axis),) + value.shape)
    return exchange(copies, axis)


def project_kernel(away, hidden_hbm, grad_hbm, in_hbm, out_hbm, terms_ref, hidden, grad, w_in, w_out, sems):
    core = lax.axis_index("core")
    core = 1 - core if away else core
    pairs, rows, lanes = terms_ref.shape
    block = pairs // CHUNKS
    dims = (((1,), (1,)), ((), ()))
    weights = [
        pltpu.make_async_copy(in_hbm, w_in, sems.at[0, CHUNKS]),
        pltpu.make_async_copy(out_hbm, w_out, sems.at[1, CHUNKS]),
    ]
    for copy in weights:
        copy.start()
    chunks = []
    for j in range(CHUNKS):
        span = pl.ds(j * block, block)
        chunks.append(
            [
                pltpu.make_async_copy(hidden_hbm.at[span, core], hidden.at[span], sems.at[0, j]),
                pltpu.make_async_copy(grad_hbm.at[span, core], grad.at[span], sems.at[1, j]),
            ]
        )
        for copy in chunks[-1]:
            copy.start()
    for copy in weights:
        copy.wait()
    for j in range(CHUNKS):
        for copy in chunks[j]:
            copy.wait()
        span = slice(j * block, (j + 1) * block)
        acts = hidden[span].reshape(block * rows, -1)
        grads = grad[span].reshape(block * rows, -1)
        left = lax.dot_general(acts, w_in[...], dims, preferred_element_type=jnp.float32)
        right = lax.dot_general(grads, w_out[...], dims, preferred_element_type=jnp.float32)
        terms_ref[span] = jnp.concatenate([left, right], axis=1).reshape(block, rows, lanes)


def project(away, hidden, grad, weights_in, weights_out):
    pairs, _, rows, wide = hidden.shape
    narrow = grad.shape[3]
    rank = weights_in.shape[0]
    operands = (hidden, grad, weights_in, weights_out)
    return pl.pallas_call(
        functools.partial(project_kernel, away),
        in_specs=[HBM, HBM, HBM, HBM],
        out_specs=VMEM,
        out_shape=jax.ShapeDtypeStruct((pairs, rows, 2 * rank), jnp.float32),
        scratch_shapes=[
            pltpu.VMEM((pairs, rows, wide), hidden.dtype),
            pltpu.VMEM((pairs, rows, narrow), grad.dtype),
            pltpu.VMEM(weights_in.shape, weights_in.dtype),
            pltpu.VMEM(weights_out.shape, weights_out.dtype),
            pltpu.SemaphoreType.DMA((2, CHUNKS + 1)),
        ],
        compiler_params=pltpu.CompilerParams(vmem_limit_bytes=16 * 1024 * 1024),
        cost_estimate=pl.CostEstimate(
            flops=2 * pairs * rows * rank * (wide + narrow),
            bytes_accessed=2 * pairs * rows * (wide + narrow) + 8 * pairs * rows * rank,
            transcendentals=0,
        ),
        name="project",
    )(*(pltpu.with_memory_space_constraint(v, pltpu.HBM) for v in operands))


def add_kernel(left_ref, right_ref, out_ref):
    out_ref[...] = left_ref[...] + right_ref[...]


def add(left, right):
    return pl.pallas_call(
        add_kernel,
        in_specs=[VMEM, VMEM],
        out_specs=VMEM,
        out_shape=jax.ShapeDtypeStruct(left.shape, left.dtype),
        compiler_params=SMALL,
        name="add",
    )(left, right)


def sketch_kernel(lengths_ref, terms_ref, out_ref):
    first = 2 * lax.axis_index(TENSOR)
    total = jnp.sum(terms_ref[...], axis=0)
    share = out_ref.shape[1] // 2
    parts = terms_ref.shape[0]
    copies = out_ref.shape[0] // parts
    seq_len, rank = total.shape[0] // 2, total.shape[1] // 2
    slot = lax.broadcasted_iota(jnp.int32, (seq_len, rank), 0)
    for s in range(2):
        mine = total[s * seq_len : (s + 1) * seq_len]
        live = (slot < lengths_ref[first + s]).astype(jnp.float32)
        sketch = contract(mine[:, :rank] * live, mine[:, rank:], ((0,), (0,)))
        mean = jnp.sum(sketch * sketch) / (rank * rank)
        unit = sketch / jnp.sqrt(jnp.full((1, 1), mean, jnp.float32) + epsilon)
        wide = jnp.concatenate([unit[: rank // 2], unit[rank // 2 :]], axis=1)
        for j in range(parts):
            piece = wide[j * share : (j + 1) * share]
            for k in range(copies):
                out_ref[k * parts + j, s * share : (s + 1) * share, :] = piece


def sketches(lengths, terms, copies):
    parts, slots, lanes = terms.shape
    rows = slots // (2 * parts)
    return pl.pallas_call(
        sketch_kernel,
        in_specs=[SMEM, VMEM],
        out_specs=VMEM,
        out_shape=jax.ShapeDtypeStruct((copies * parts, 2 * rows, lanes), jnp.float32),
        compiler_params=SMALL,
        name="sketches",
    )(lengths, terms)


def gram_kernel(own_ref, other_ref, cols_ref, out_ref, rows, held):
    parts, blocks, lanes = out_ref.shape
    share = rows.shape[0]
    first = lax.axis_index("core") == 0
    own, other = own_ref[...], other_ref[...]
    held[0] = jnp.where(first, own, other)
    held[1] = jnp.where(first, other, own)
    for core in range(2):
        for s in range(2):
            for r in range(share):
                rows[r, pl.ds(2 * core + s, parts, stride=4), :] = held[
                    core, pl.ds(s * share + r, parts, stride=2 * share), :
                ]
    halves = []
    for s in range(2):
        total = jnp.zeros((parts * blocks, lanes // 2), jnp.float32)
        for r in range(share):
            left = cols_ref[pl.ds(s * share + r, parts * blocks, stride=2 * share), :]
            total = total + contract(left, rows[r], ((1,), (1,)))
        halves.append(total)
    both = jnp.concatenate(halves, axis=1).reshape(blocks, parts, lanes)
    for b in range(blocks):
        out_ref[:, b, :] = both[b]


def gram(own, other, cols, parts, blocks):
    n_slots, lanes = own.shape
    share = n_slots // (2 * parts)
    return pl.pallas_call(
        gram_kernel,
        in_specs=[VMEM, VMEM, VMEM],
        out_specs=VMEM,
        out_shape=jax.ShapeDtypeStruct((parts, blocks, 2 * 4 * parts), jnp.float32),
        scratch_shapes=[
            pltpu.VMEM((share, 4 * parts, lanes), jnp.float32),
            pltpu.VMEM((2, n_slots, lanes), jnp.float32),
        ],
        compiler_params=SMALL,
        name="gram",
    )(own, other, cols)


def finish_kernel(tasks_ref, terms_ref, out_ref):
    group = lax.axis_index(DP)
    n_y, n_z, seqs = 4, 4, out_ref.shape[2]
    total = jnp.sum(terms_ref[...], axis=0) * (1.0 / seqs)
    for y in range(n_y):
        for k in range(n_z):
            z = k
            block = z * n_y + y
            same = tasks_ref[block] == tasks_ref[group]
            row = total[y * n_z + k : y * n_z + k + 1]
            row = jnp.where(same, row, jnp.float32(0.0))
            out_ref[block] = jnp.concatenate([row[:, :seqs], row[:, seqs:]], axis=0)


def finish(tasks, terms):
    _, groups, lanes = terms.shape
    return pl.pallas_call(
        finish_kernel,
        in_specs=[SMEM, VMEM],
        out_specs=VMEM,
        out_shape=jax.ShapeDtypeStruct((groups, 2, lanes // 2), jnp.float32),
        compiler_params=SMALL,
        name="finish",
    )(tasks, terms)


def body(hidden, out_grad, proj_in, proj_out, lengths, task_ids):
    block_rows, seq_len, _ = hidden.shape
    rank = proj_in.shape[1]
    groups = lax.axis_size(DP)
    chips = lax.axis_size(CHIPS)
    share = block_rows // lax.axis_size(TENSOR)
    pair_rows = share * seq_len

    hidden = hidden.reshape(chips, 2, pair_rows, -1)
    out_grad = out_grad.reshape(chips, 2, pair_rows, -1)
    weights = (proj_in.T, proj_out.T)
    send = project(True, hidden, out_grad, *weights)
    keep = project(False, hidden, out_grad, *weights)
    mine = add(keep, lax.ppermute(send, "core", [(0, 1), (1, 0)]))
    terms = exchange(mine, CHIPS)
    n_z = lax.axis_size("z_hi")
    units = sketches(lengths, terms, n_z)
    spread = exchange(units, ("z_hi",) + CHIPS).reshape(n_z, -1, 2 * rank)
    mine = lax.dynamic_index_in_dim(spread, lax.axis_index("z_hi"), 0, keepdims=False)
    other = lax.ppermute(mine, "core", [(0, 1), (1, 0)])
    cols = gather(spread, "y").reshape(-1, 2 * rank)
    partial_value = gram(mine, other, cols, chips, groups)
    return finish(task_ids, exchange(partial_value, CHIPS)).transpose(2, 0, 1)


def solution(mesh):
    fine = Mesh(np.asarray(mesh.devices).reshape(SIZES), AXES)
    in_specs = (
        P(DP, None, TENSOR),
        P(DP, None, TENSOR),
        P(TENSOR, None),
        P(TENSOR, None),
        P(DP),
        P(),
    )
    out_specs = P(DP, None, TENSOR)
    return jax.shard_map(body, mesh=fine, in_specs=in_specs, out_specs=out_specs, check_vma=False)
```

time: 102 us -> 90.9 us (0.89)
  the two profiles are of different devices: /device:TPU:1 before, /device:TPU:2 now
where the time goes in v2:
time: 90.9 us; the launch traced here: 90.6 us
  blocking collectives  66.9 us (74%)
  Pallas kernels  8.31 us (9%)
  starting transfers between devices  8.29 us (9%)
  waiting for transfers between devices  6.17 us (7%)
    all_to_all x3, blocking collectives, exchange(): return lax.all_to_all(value, axes, 0, 0, tiled=True)  66.9 us
    pallas_call x2, Pallas kernels, project(): pl.pallas_call(functools.partial(project_kernel, away), in_specs=[HBM, HB...  5.24 us
    all_to_all x1, waiting for transfers between devices, exchange(): return lax.all_to_all(value, axes, 0, 0, tiled=True)  4.99 us
    all_to_all x1, starting transfers between devices, exchange(): return lax.all_to_all(value, axes, 0, 0, tiled=True)  4.46 us
    ppermute x1, starting transfers between devices, body(): mine = add(keep, lax.ppermute(send, 'core', [(0, 1), (1, 0)]))  1.92 us
    ppermute x1, starting transfers between devices, body(): other = lax.ppermute(mine, 'core', [(0, 1), (1, 0)])  1.91 us
  transfers between devices with their start and end apart: 3, of which 2 were waited for; matrix products, arithmetic and copies ran while one was open for 0% of the time, Pallas kernels for 3%

profile of v2, /device:TPU:2, one launch (start us, length us, event | category | flops | bytes accessed | tf_op | source)
XLA Modules:
  0.0 90.6 jit_solution(2628193920614643263)
XLA Ops:
  0.0 2.6 %project.3 = f32[16,64,128]{2,1,0:T(8,128)S(1)} custom-call(bf16[16,2,64,896]{3,2,1,0:T(8,128)(2,1)} %bitcast.10, bf16[16,2,64,256]{3,2,1,0:T(8,128)(2,1)} %bitcast.12, bf16[64,896]{1,0:T(8,128)(2,1)} %bitcast.16, bf16[64,256]{1,0:T(8,128)(2,1)} %bitcast.18), custom_call_target="tpu_custom_call" | custom-call | flops 150994944 | bytes 2883584 | tf_op jit(solution)/shard_map/project/pallas_call | solution.py:84
  2.6 0.0 copy-start.1
  2.6 1.9 %collective-permute-start = (f32[16,64,128]{2,1,0:T(8,128)S(1)}, f32[16,64,128]{2,1,0:T(8,128)S(1)}, u32[]{:S(2)}, u32[]{:S(2)}) collective-permute-start(f32[16,64,128]{2,1,0:T(8,128)S(1)} %project.3), channel_id=1, source_target_pairs={{0,1},{1,0},{2,3},{3,2},{4,5},{5,4},{6,7},{7,6},{8,9},{9,8},{10,11... | collective-permute-start | bytes 1572872 | tf_op jit(solution)/shard_map/ppermute | solution.py:236
  4.6 2.6 %project.2.left_ref = f32[16,64,128]{2,1,0:T(8,128)S(1)} custom-call(bf16[16,2,64,896]{3,2,1,0:T(8,128)(2,1)} %bitcast.11, bf16[16,2,64,256]{3,2,1,0:T(8,128)(2,1)} %bitcast.13, bf16[64,896]{1,0:T(8,128)(2,1)} %bitcast.17, bf16[64,256]{1,0:T(8,128)(2,1)} %bitcast.19), custom_call_target="tpu_custom_call" | custom-call | flops 150994944 | bytes 2883584 | tf_op jit(solution)/shard_map/project/pallas_call | solution.py:84
  7.2 0.0 copy-start
  7.2 0.0 collective-permute-done.right_ref
  7.2 0.1 add.6
  7.3 23.1 %all_to_all.20.terms_ref = f32[16,64,128]{2,1,0:T(8,128)S(1)} all-to-all(f32[16,64,128]{2,1,0:T(8,128)S(1)} %add.6), channel_id=1, replica_groups=mesh['z_hi'=4,'y'=4,'z_lo'=4,'x'=4,'core'=2] {'z_lo','x'}, dimensions={0} | all-to-all | bytes 1048576 | tf_op jit(solution)/shard_map/all_to_all | solution.py:35
  30.4 0.0 copy-done.1
  30.4 1.1 %sketches.1 = f32[64,4,128]{2,1,0:T(4,128)S(1)} custom-call(s32[64]{0:T(128)S(1)} %copy-done.1, f32[16,64,128]{2,1,0:T(8,128)S(1)} %all_to_all.20.terms_ref), custom_call_target="tpu_custom_call" | custom-call | tf_op jit(solution)/shard_map/sketches/pallas_call | solution.py:145
  31.4 31.7 %all_to_all.21 = f32[64,4,128]{2,1,0:T(4,128)S(1)} all-to-all(f32[64,4,128]{2,1,0:T(4,128)S(1)} %sketches.1), channel_id=1, replica_groups=mesh['z_hi'=4,'y'=4,'z_lo'=4,'x'=4,'core'=2] {'z_hi','z_lo','x'}, dimensions={0} | all-to-all | bytes 262144 | tf_op jit(solution)/shard_map/all_to_all | solution.py:35
  63.2 0.8 broadcast_in_dim.2
  64.0 4.5 %all-to-all-start.2 = ((f32[4,4,64,128]{3,2,1,0:T(8,128)}), f32[4,4,64,128]{3,2,1,0:T(8,128)S(1)}, u32[]{:S(2)}, u32[]{:S(2)}) async-start(f32[4,4,64,128]{3,2,1,0:T(8,128)} %broadcast_in_dim.2), calls=%async_computation.2 | async-start | bytes 1048576 | tf_op jit(solution)/shard_map/all_to_all | solution.py:35
  68.5 1.9 %collective-permute-start.1 = (f32[64,128]{1,0:T(8,128)S(1)}, f32[64,128]{1,0:T(8,128)S(1)}, u32[]{:S(2)}, u32[]{:S(2)}) collective-permute-start(f32[64,128]{1,0:T(8,128)S(1)} %dynamic-slice_bitcast_fusion.own_ref), channel_id=1, source_target_pairs={{0,1},{1,0},{2,3},{3,2},{4,5},{5,4},{6,7},{7,6},{8,9},{9,8},{10,11... | collective-permute-start | bytes 98312 | tf_op jit(solution)/shard_map/ppermute | solution.py:242
  70.4 1.2 %collective-permute-done.1.other_ref = f32[64,128]{1,0:T(8,128)S(1)} collective-permute-done((f32[64,128]{1,0:T(8,128)S(1)}, f32[64,128]{1,0:T(8,128)S(1)}, u32[]{:S(2)}, u32[]{:S(2)}) %collective-permute-start.1) | collective-permute-done | bytes 32800 | tf_op jit(solution)/shard_map/ppermute | solution.py:242
  71.5 5.0 %all-to-all-done.2 = f32[4,4,64,128]{3,2,1,0:T(8,128)S(1)} async-done(((f32[4,4,64,128]{3,2,1,0:T(8,128)}), f32[4,4,64,128]{3,2,1,0:T(8,128)S(1)}, u32[]{:S(2)}, u32[]{:S(2)}) %all-to-all-start.2) | async-done | bytes 524320 | tf_op jit(solution)/shard_map/all_to_all | solution.py:35
  76.5 0.7 gram.1
  77.2 12.1 %all_to_all.22.terms_ref = f32[16,16,128]{2,1,0:T(8,128)S(1)} all-to-all(f32[16,16,128]{2,1,0:T(8,128)S(1)} %gram.1), channel_id=1, replica_groups=mesh['z_hi'=4,'y'=4,'z_lo'=4,'x'=4,'core'=2] {'z_lo','x'}, dimensions={0} | all-to-all | bytes 262144 | tf_op jit(solution)/shard_map/all_to_all | solution.py:35
  89.3 0.0 copy-done
  89.3 1.3 %finish.1 = f32[16,2,64]{2,1,0:T(2,128)} custom-call(s32[16]{0:T(128)S(1)} %copy-done, f32[16,16,128]{2,1,0:T(8,128)S(1)} %all_to_all.22.terms_ref), custom_call_target="tpu_custom_call" | custom-call | tf_op jit(solution)/shard_map/finish/pallas_call | solution.py:213
  (1 shorter events, 0.0 us)
Async XLA Ops:
  2.6 27.7 %copy-start.1 = (s32[64]{0:T(128)S(1)}, s32[64]{0:T(128)}, u32[]{:S(2)}) copy-start(s32[64]{0:T(128)} %lengths_ref.1) | copy-start | bytes 772
  2.6 4.6 %collective-permute-start = (f32[16,64,128]{2,1,0:T(8,128)S(1)}, f32[16,64,128]{2,1,0:T(8,128)S(1)}, u32[]{:S(2)}, u32[]{:S(2)}) collective-permute-start(f32[16,64,128]{2,1,0:T(8,128)S(1)} %project.3), channel_id=1, source_target_pairs={{0,1},{1,0},{2,3},{3,2},{4,5},{5,4},{6,7},{7,6},{8,9},{9,8},{10,11... | collective-permute-start | bytes 1572872 | tf_op jit(solution)/shard_map/ppermute | solution.py:236
  7.2 82.1 %copy-start = (s32[16]{0:T(128)S(1)}, s32[16]{0:T(128)}, u32[]{:S(2)}) copy-start(s32[16]{0:T(128)} %tasks_ref.1) | copy-start | bytes 196
  64.0 12.5 %all-to-all-start.2 = ((f32[4,4,64,128]{3,2,1,0:T(8,128)}), f32[4,4,64,128]{3,2,1,0:T(8,128)S(1)}, u32[]{:S(2)}, u32[]{:S(2)}) async-start(f32[4,4,64,128]{3,2,1,0:T(8,128)} %broadcast_in_dim.2), calls=%async_computation.2 | async-start | bytes 1048576 | tf_op jit(solution)/shard_map/all_to_all | solution.py:35
  68.5 3.1 %collective-permute-start.1 = (f32[64,128]{1,0:T(8,128)S(1)}, f32[64,128]{1,0:T(8,128)S(1)}, u32[]{:S(2)}, u32[]{:S(2)}) collective-permute-start(f32[64,128]{1,0:T(8,128)S(1)} %dynamic-slice_bitcast_fusion.own_ref), channel_id=1, source_target_pairs={{0,1},{1,0},{2,3},{3,2},{4,5},{5,4},{6,7},{7,6},{8,9},{9,8},{10,11... | collective-permute-start | bytes 98312 | tf_op jit(solution)/shard_map/ppermute | solution.py:242

commit v3 on v2

--- a/solution.py
+++ b/solution.py
@@ -1,5 +1,3 @@
-import functools
-
 import jax
 import jax.numpy as jnp
 import numpy as np
@@ -19,7 +17,6 @@
 
 HIGHEST = lax.Precision.HIGHEST
 VMEM = pl.BlockSpec(memory_space=pltpu.VMEM)
-SMEM = pl.BlockSpec(memory_space=pltpu.SMEM)
 CHUNKS = 4
 HBM = pl.BlockSpec(memory_space=pltpu.HBM)
 SMALL = pltpu.CompilerParams(vmem_limit_bytes=8 * 1024 * 1024)
@@ -40,9 +37,8 @@
     return exchange(copies, axis)
 
 
-def project_kernel(away, hidden_hbm, grad_hbm, in_hbm, out_hbm, terms_ref, hidden, grad, w_in, w_out, sems):
-    core = lax.axis_index("core")
-    core = 1 - core if away else core
+def project_kernel(hidden_hbm, grad_hbm, in_hbm, out_hbm, terms_ref, hidden, grad, w_in, w_out, sems):
+    core = 1 - lax.axis_index("core")
     pairs, rows, lanes = terms_ref.shape
     block = pairs // CHUNKS
     dims = (((1,), (1,)), ((), ()))
@@ -76,13 +72,13 @@
         terms_ref[span] = jnp.concatenate([left, right], axis=1).reshape(block, rows, lanes)
 
 
-def project(away, hidden, grad, weights_in, weights_out):
+def project(hidden, grad, weights_in, weights_out):
     pairs, _, rows, wide = hidden.shape
     narrow = grad.shape[3]
     rank = weights_in.shape[0]
     operands = (hidden, grad, weights_in, weights_out)
     return pl.pallas_call(
-        functools.partial(project_kernel, away),
+        project_kernel,
         in_specs=[HBM, HBM, HBM, HBM],
         out_specs=VMEM,
         out_shape=jax.ShapeDtypeStruct((pairs, rows, 2 * rank), jnp.float32),
@@ -103,6 +99,38 @@
     )(*(pltpu.with_memory_space_constraint(v, pltpu.HBM) for v in operands))
 
 
+def rest_kernel(hidden_ref, grad_ref, in_ref, out_ref, terms_ref):
+    core = lax.axis_index("core")
+    pairs, rows, lanes = terms_ref.shape
+    block = pairs // CHUNKS
+    dims = (((1,), (1,)), ((), ()))
+    for j in range(CHUNKS):
+        span = slice(j * block, (j + 1) * block)
+        acts = hidden_ref[span, core].reshape(block * rows, -1)
+        grads = grad_ref[span, core].reshape(block * rows, -1)
+        left = lax.dot_general(acts, in_ref[...], dims, preferred_element_type=jnp.float32)
+        right = lax.dot_general(grads, out_ref[...], dims, preferred_element_type=jnp.float32)
+        terms_ref[span] = jnp.concatenate([left, right], axis=1).reshape(block, rows, lanes)
+
+
+def project_rest(hidden, grad, weights_in, weights_out):
+    pairs, _, rows, wide = hidden.shape
+    rank = weights_in.shape[0]
+    return pl.pallas_call(
+        rest_kernel,
+        in_specs=[VMEM, VMEM, VMEM, VMEM],
+        out_specs=VMEM,
+        out_shape=jax.ShapeDtypeStruct((pairs, rows, 2 * rank), jnp.float32),
+        compiler_params=pltpu.CompilerParams(vmem_limit_bytes=16 * 1024 * 1024),
+        cost_estimate=pl.CostEstimate(
+            flops=2 * pairs * rows * rank * (wide + grad.shape[3]),
+            bytes_accessed=8 * pairs * rows * rank,
+            transcendentals=0,
+        ),
+        name="project_rest",
+    )(hidden, grad, weights_in, weights_out)
+
+
 def add_kernel(left_ref, right_ref, out_ref):
     out_ref[...] = left_ref[...] + right_ref[...]
 
@@ -126,9 +154,12 @@
     copies = out_ref.shape[0] // parts
     seq_len, rank = total.shape[0] // 2, total.shape[1] // 2
     slot = lax.broadcasted_iota(jnp.int32, (seq_len, rank), 0)
+    lengths = lengths_ref[...]
+    lane = lax.broadcasted_iota(jnp.int32, lengths.shape, 1)
     for s in range(2):
         mine = total[s * seq_len : (s + 1) * seq_len]
-        live = (slot < lengths_ref[first + s]).astype(jnp.float32)
+        length = jnp.sum(jnp.where(lane == first + s, lengths, 0), axis=1, keepdims=True)
+        live = (slot < length).astype(jnp.float32)
         sketch = contract(mine[:, :rank] * live, mine[:, rank:], ((0,), (0,)))
         mean = jnp.sum(sketch * sketch) / (rank * rank)
         unit = sketch / jnp.sqrt(jnp.full((1, 1), mean, jnp.float32) + epsilon)
@@ -144,12 +175,12 @@
     rows = slots // (2 * parts)
     return pl.pallas_call(
         sketch_kernel,
-        in_specs=[SMEM, VMEM],
+        in_specs=[VMEM, VMEM],
         out_specs=VMEM,
         out_shape=jax.ShapeDtypeStruct((copies * parts, 2 * rows, lanes), jnp.float32),
         compiler_params=SMALL,
         name="sketches",
-    )(lengths, terms)
+    )(lengths[None], terms)
 
 
 def gram_kernel(own_ref, other_ref, cols_ref, out_ref, rows, held):
@@ -198,26 +229,32 @@
     group = lax.axis_index(DP)
     n_y, n_z, seqs = 4, 4, out_ref.shape[2]
     total = jnp.sum(terms_ref[...], axis=0) * (1.0 / seqs)
+    tasks = tasks_ref[...]
+    lane = lax.broadcasted_iota(jnp.int32, tasks.shape, 1)
+    own = jnp.sum(jnp.where(lane == group, tasks, 0), axis=1, keepdims=True)
+    same = jnp.where(tasks == own, 1.0, 0.0)
+    blocks = out_ref.shape[0]
+    row = lax.broadcasted_iota(jnp.int32, (blocks, blocks), 0)
+    col = lax.broadcasted_iota(jnp.int32, (blocks, blocks), 1)
+    hit = row % n_z * n_y + row // n_z == col
+    live = jnp.sum(jnp.where(hit, jnp.broadcast_to(same, (blocks, blocks)), 0.0), axis=1, keepdims=True)
+    total = jnp.where(live > 0.5, total, 0.0)
     for y in range(n_y):
-        for k in range(n_z):
-            z = k
-            block = z * n_y + y
-            same = tasks_ref[block] == tasks_ref[group]
-            row = total[y * n_z + k : y * n_z + k + 1]
-            row = jnp.where(same, row, jnp.float32(0.0))
-            out_ref[block] = jnp.concatenate([row[:, :seqs], row[:, seqs:]], axis=0)
+        for z in range(n_z):
+            line = total[y * n_z + z : y * n_z + z + 1]
+            out_ref[z * n_y + y] = jnp.concatenate([line[:, :seqs], line[:, seqs:]], axis=0)
 
 
 def finish(tasks, terms):
     _, groups, lanes = terms.shape
     return pl.pallas_call(
         finish_kernel,
-        in_specs=[SMEM, VMEM],
+        in_specs=[VMEM, VMEM],
         out_specs=VMEM,
         out_shape=jax.ShapeDtypeStruct((groups, 2, lanes // 2), jnp.float32),
         compiler_params=SMALL,
         name="finish",
-    )(tasks, terms)
+    )(tasks[None], terms)
 
 
 def body(hidden, out_grad, proj_in, proj_out, lengths, task_ids):
@@ -231,8 +268,8 @@
     hidden = hidden.reshape(chips, 2, pair_rows, -1)
     out_grad = out_grad.reshape(chips, 2, pair_rows, -1)
     weights = (proj_in.T, proj_out.T)
-    send = project(True, hidden, out_grad, *weights)
-    keep = project(False, hidden, out_grad, *weights)
+    send = project(hidden, out_grad, *weights)
+    keep = project_rest(hidden, out_grad, *weights)
     mine = add(keep, lax.ppermute(send, "core", [(0, 1), (1, 0)]))
     terms = exchange(mine, CHIPS)
     n_z = lax.axis_size("z_hi")

time: 90.9 us -> 88.5 us (0.974)
  Pallas kernels: 8.31 us -> 5.78 us
  blocking collectives: 66.9 us -> 65.9 us
  waiting for transfers between devices: 6.17 us -> 7.16 us
    pallas_call x4, Pallas kernels: 7.55 us -> 5.02 us  [the longest x1 2.76 us: project(): pl.pallas_call(project_kernel, in_specs=[HBM, HBM, HBM, HBM], out_specs=V...]
    ppermute x1, waiting for transfers between devices: 0.01 us -> 1 us  [body(): mine = add(keep, lax.ppermute(send, 'core', [(0, 1), (1, 0)]))]
    all_to_all x3, blocking collectives: 66.9 us -> 65.9 us  [exchange(): return lax.all_to_all(value, axes, 0, 0, tiled=True)]
  transfers between devices with their start and end apart: 3 -> 3, of which waited for: 2 -> 3; matrix products, arithmetic and copies ran while one was open for 0% -> 0% of each run, Pallas kernels for 3% -> 1%
where the time goes in v3:
time: 88.5 us; the launch traced here: 88.2 us
  blocking collectives  65.9 us (74%)
  starting transfers between devices  8.29 us (9%)
  waiting for transfers between devices  7.16 us (8%)
  Pallas kernels  5.78 us (7%)
    all_to_all x3, blocking collectives, exchange(): return lax.all_to_all(value, axes, 0, 0, tiled=True)  65.9 us
    all_to_all x1, waiting for transfers between devices, exchange(): return lax.all_to_all(value, axes, 0, 0, tiled=True)  4.99 us
    all_to_all x1, starting transfers between devices, exchange(): return lax.all_to_all(value, axes, 0, 0, tiled=True)  4.47 us
    pallas_call x1, Pallas kernels, project(): pl.pallas_call(project_kernel, in_specs=[HBM, HBM, HBM, HBM], out_specs=V...  2.76 us
    ppermute x1, starting transfers between devices, body(): mine = add(keep, lax.ppermute(send, 'core', [(0, 1), (1, 0)]))  1.92 us
    ppermute x1, starting transfers between devices, body(): other = lax.ppermute(mine, 'core', [(0, 1), (1, 0)])  1.91 us
  transfers between devices with their start and end apart: 3, of which 3 were waited for; matrix products, arithmetic and copies ran while one was open for 0% of the time, Pallas kernels for 1%

profile of v3, /device:TPU:2, one launch (start us, length us, event | category | flops | bytes accessed | tf_op | source)
XLA Modules:
  0.0 88.2 jit_solution(16935990124593423730)
XLA Ops:
  0.0 0.0 copy-start.3
  0.0 2.8 %project.1 = f32[16,64,128]{2,1,0:T(8,128)S(1)} custom-call(bf16[16,2,64,896]{3,2,1,0:T(8,128)(2,1)} %bitcast.11, bf16[16,2,64,256]{3,2,1,0:T(8,128)(2,1)} %bitcast.13, bf16[64,896]{1,0:T(8,128)(2,1)} %bitcast.16, bf16[64,256]{1,0:T(8,128)(2,1)} %bitcast.18), custom_call_target="tpu_custom_call" | custom-call | flops 150994944 | bytes 2883584 | tf_op jit(solution)/shard_map/project/pallas_call | solution.py:80
  2.8 0.0 copy-start.5
  2.8 1.9 %collective-permute-start = (f32[16,64,128]{2,1,0:T(8,128)S(1)}, f32[16,64,128]{2,1,0:T(8,128)S(1)}, u32[]{:S(2)}, u32[]{:S(2)}) collective-permute-start(f32[16,64,128]{2,1,0:T(8,128)S(1)} %project.1), channel_id=1, source_target_pairs={{0,1},{1,0},{2,3},{3,2},{4,5},{5,4},{6,7},{7,6},{8,9},{9,8},{10,11... | collective-permute-start | bytes 1572872 | tf_op jit(solution)/shard_map/ppermute | solution.py:273
  4.7 0.0 copy-done
  4.7 0.0 copy-done.1
  4.7 0.0 copy-done.2
  4.8 0.0 copy-done.3
  4.8 0.8 project_rest.1.left_ref
  5.6 0.0 copy-start.4
  5.6 1.0 %collective-permute-done.right_ref = f32[16,64,128]{2,1,0:T(8,128)S(1)} collective-permute-done((f32[16,64,128]{2,1,0:T(8,128)S(1)}, f32[16,64,128]{2,1,0:T(8,128)S(1)}, u32[]{:S(2)}, u32[]{:S(2)}) %collective-permute-start) | collective-permute-done | bytes 524320 | tf_op jit(solution)/shard_map/ppermute | solution.py:273
  6.6 0.1 add.6
  6.7 22.9 %all_to_all.20.terms_ref = f32[16,64,128]{2,1,0:T(8,128)S(1)} all-to-all(f32[16,64,128]{2,1,0:T(8,128)S(1)} %add.6), channel_id=1, replica_groups=mesh['z_hi'=4,'y'=4,'z_lo'=4,'x'=4,'core'=2] {'z_lo','x'}, dimensions={0} | all-to-all | bytes 1048576 | tf_op jit(solution)/shard_map/all_to_all | solution.py:32
  29.5 0.0 copy-done.5
  29.5 0.6 sketches.1
  30.1 31.1 %all_to_all.21 = f32[64,4,128]{2,1,0:T(4,128)S(1)} all-to-all(f32[64,4,128]{2,1,0:T(4,128)S(1)} %sketches.1), channel_id=1, replica_groups=mesh['z_hi'=4,'y'=4,'z_lo'=4,'x'=4,'core'=2] {'z_hi','z_lo','x'}, dimensions={0} | all-to-all | bytes 262144 | tf_op jit(solution)/shard_map/all_to_all | solution.py:32
  61.2 0.9 broadcast_in_dim.13
  62.1 4.5 %all-to-all-start.2 = ((f32[4,4,64,128]{3,2,1,0:T(8,128)}), f32[4,4,64,128]{3,2,1,0:T(8,128)S(1)}, u32[]{:S(2)}, u32[]{:S(2)}) async-start(f32[4,4,64,128]{3,2,1,0:T(8,128)} %broadcast_in_dim.13), calls=%async_computation.2 | async-start | bytes 1048576 | tf_op jit(solution)/shard_map/all_to_all | solution.py:32
  66.6 1.9 %collective-permute-start.1 = (f32[64,128]{1,0:T(8,128)S(1)}, f32[64,128]{1,0:T(8,128)S(1)}, u32[]{:S(2)}, u32[]{:S(2)}) collective-permute-start(f32[64,128]{1,0:T(8,128)S(1)} %dynamic-slice_bitcast_fusion.own_ref), channel_id=1, source_target_pairs={{0,1},{1,0},{2,3},{3,2},{4,5},{5,4},{6,7},{7,6},{8,9},{9,8},{10,11... | collective-permute-start | bytes 98312 | tf_op jit(solution)/shard_map/ppermute | solution.py:279
  68.5 1.2 %collective-permute-done.1.other_ref = f32[64,128]{1,0:T(8,128)S(1)} collective-permute-done((f32[64,128]{1,0:T(8,128)S(1)}, f32[64,128]{1,0:T(8,128)S(1)}, u32[]{:S(2)}, u32[]{:S(2)}) %collective-permute-start.1) | collective-permute-done | bytes 32800 | tf_op jit(solution)/shard_map/ppermute | solution.py:279
  69.6 5.0 %all-to-all-done.2 = f32[4,4,64,128]{3,2,1,0:T(8,128)S(1)} async-done(((f32[4,4,64,128]{3,2,1,0:T(8,128)}), f32[4,4,64,128]{3,2,1,0:T(8,128)S(1)}, u32[]{:S(2)}, u32[]{:S(2)}) %all-to-all-start.2) | async-done | bytes 524320 | tf_op jit(solution)/shard_map/all_to_all | solution.py:32
  74.6 0.7 gram.1
  75.3 12.0 %all_to_all.22.terms_ref = f32[16,16,128]{2,1,0:T(8,128)S(1)} all-to-all(f32[16,16,128]{2,1,0:T(8,128)S(1)} %gram.1), channel_id=1, replica_groups=mesh['z_hi'=4,'y'=4,'z_lo'=4,'x'=4,'core'=2] {'z_lo','x'}, dimensions={0} | all-to-all | bytes 262144 | tf_op jit(solution)/shard_map/all_to_all | solution.py:32
  87.3 0.9 finish.1
  (5 shorter events, 0.0 us)
Async XLA Ops:
  0.0 4.7 %copy-start = (bf16[64,32,896]{2,1,0:T(8,128)(2,1)S(1)}, bf16[64,32,896]{2,1,0:T(8,128)(2,1)}, u32[]{:S(2)}) copy-start(bf16[64,32,896]{2,1,0:T(8,128)(2,1)} %param.6) | copy-start | bytes 11010052
  0.0 4.7 %copy-start.1 = (bf16[64,32,256]{2,1,0:T(8,128)(2,1)S(1)}, bf16[64,32,256]{2,1,0:T(8,128)(2,1)}, u32[]{:S(2)}) copy-start(bf16[64,32,256]{2,1,0:T(8,128)(2,1)} %param.7) | copy-start | bytes 3145732
  0.0 4.7 %copy-start.2 = (bf16[896,64]{0,1:T(8,128)(2,1)S(1)}, bf16[896,64]{0,1:T(8,128)(2,1)}, u32[]{:S(2)}) copy-start(bf16[896,64]{0,1:T(8,128)(2,1)} %param.8) | copy-start | bytes 344068
  0.0 4.8 %copy-start.3 = (bf16[256,64]{0,1:T(8,128)(2,1)S(1)}, bf16[256,64]{0,1:T(8,128)(2,1)}, u32[]{:S(2)}) copy-start(bf16[256,64]{0,1:T(8,128)(2,1)} %param.9) | copy-start | bytes 98308
  2.8 26.7 %copy-start.5 = (s32[64]{0:T(128)S(1)}, s32[64]{0:T(128)}, u32[]{:S(2)}) copy-start(s32[64]{0:T(128)} %param.10) | copy-start | bytes 772
  2.8 3.8 %collective-permute-start = (f32[16,64,128]{2,1,0:T(8,128)S(1)}, f32[16,64,128]{2,1,0:T(8,128)S(1)}, u32[]{:S(2)}, u32[]{:S(2)}) collective-permute-start(f32[16,64,128]{2,1,0:T(8,128)S(1)} %project.1), channel_id=1, source_target_pairs={{0,1},{1,0},{2,3},{3,2},{4,5},{5,4},{6,7},{7,6},{8,9},{9,8},{10,11... | collective-permute-start | bytes 1572872 | tf_op jit(solution)/shard_map/ppermute | solution.py:273
  5.6 81.7 %copy-start.4 = (s32[16]{0:T(128)S(1)}, s32[16]{0:T(128)}, u32[]{:S(2)}) copy-start(s32[16]{0:T(128)} %param.11) | copy-start | bytes 196
  62.1 12.5 %all-to-all-start.2 = ((f32[4,4,64,128]{3,2,1,0:T(8,128)}), f32[4,4,64,128]{3,2,1,0:T(8,128)S(1)}, u32[]{:S(2)}, u32[]{:S(2)}) async-start(f32[4,4,64,128]{3,2,1,0:T(8,128)} %broadcast_in_dim.13), calls=%async_computation.2 | async-start | bytes 1048576 | tf_op jit(solution)/shard_map/all_to_all | solution.py:32
  66.6 3.1 %collective-permute-start.1 = (f32[64,128]{1,0:T(8,128)S(1)}, f32[64,128]{1,0:T(8,128)S(1)}, u32[]{:S(2)}, u32[]{:S(2)}) collective-permute-start(f32[64,128]{1,0:T(8,128)S(1)} %dynamic-slice_bitcast_fusion.own_ref), channel_id=1, source_target_pairs={{0,1},{1,0},{2,3},{3,2},{4,5},{5,4},{6,7},{7,6},{8,9},{9,8},{10,11... | collective-permute-start | bytes 98312 | tf_op jit(solution)/shard_map/ppermute | solution.py:279

commit v4 on v3

--- a/solution.py
+++ b/solution.py
@@ -17,7 +17,7 @@
 
 HIGHEST = lax.Precision.HIGHEST
 VMEM = pl.BlockSpec(memory_space=pltpu.VMEM)
-CHUNKS = 4
+CHUNKS = 2
 HBM = pl.BlockSpec(memory_space=pltpu.HBM)
 SMALL = pltpu.CompilerParams(vmem_limit_bytes=8 * 1024 * 1024)
 

time: 88.5 us -> 88.3 us (level)
  no operation moved by 1% of the time
where the time goes in v4:
time: 88.3 us; the launch traced here: 88 us
  blocking collectives  66 us (75%)
  starting transfers between devices  8.29 us (9%)
  waiting for transfers between devices  7.16 us (8%)
  Pallas kernels  5.63 us (6%)
    all_to_all x3, blocking collectives, exchange(): return lax.all_to_all(value, axes, 0, 0, tiled=True)  66 us
    all_to_all x1, waiting for transfers between devices, exchange(): return lax.all_to_all(value, axes, 0, 0, tiled=True)  4.99 us
    all_to_all x1, starting transfers between devices, exchange(): return lax.all_to_all(value, axes, 0, 0, tiled=True)  4.47 us
    pallas_call x1, Pallas kernels, project(): pl.pallas_call(project_kernel, in_specs=[HBM, HBM, HBM, HBM], out_specs=V...  2.61 us
    ppermute x1, starting transfers between devices, body(): mine = add(keep, lax.ppermute(send, 'core', [(0, 1), (1, 0)]))  1.92 us
    ppermute x1, starting transfers between devices, body(): other = lax.ppermute(mine, 'core', [(0, 1), (1, 0)])  1.91 us
  transfers between devices with their start and end apart: 3, of which 3 were waited for; matrix products, arithmetic and copies ran while one was open for 0% of the time, Pallas kernels for 1%

profile of v4, /device:TPU:2, one launch (start us, length us, event | category | flops | bytes accessed | tf_op | source)
XLA Modules:
  0.0 88.0 jit_solution(1477059280297529507)
XLA Ops:
  0.0 0.0 copy-start.3
  0.0 2.6 %project.1 = f32[16,64,128]{2,1,0:T(8,128)S(1)} custom-call(bf16[16,2,64,896]{3,2,1,0:T(8,128)(2,1)} %bitcast.11, bf16[16,2,64,256]{3,2,1,0:T(8,128)(2,1)} %bitcast.13, bf16[64,896]{1,0:T(8,128)(2,1)} %bitcast.16, bf16[64,256]{1,0:T(8,128)(2,1)} %bitcast.18), custom_call_target="tpu_custom_call" | custom-call | flops 150994944 | bytes 2883584 | tf_op jit(solution)/shard_map/project/pallas_call | solution.py:80
  2.6 0.0 copy-start.5
  2.6 1.9 %collective-permute-start = (f32[16,64,128]{2,1,0:T(8,128)S(1)}, f32[16,64,128]{2,1,0:T(8,128)S(1)}, u32[]{:S(2)}, u32[]{:S(2)}) collective-permute-start(f32[16,64,128]{2,1,0:T(8,128)S(1)} %project.1), channel_id=1, source_target_pairs={{0,1},{1,0},{2,3},{3,2},{4,5},{5,4},{6,7},{7,6},{8,9},{9,8},{10,11... | collective-permute-start | bytes 1572872 | tf_op jit(solution)/shard_map/ppermute | solution.py:273
  4.6 0.0 copy-done
  4.6 0.0 copy-done.1
  4.6 0.0 copy-done.2
  4.6 0.0 copy-done.3
  4.6 0.8 project_rest.1.left_ref
  5.4 0.0 copy-start.4
  5.5 1.0 %collective-permute-done.right_ref = f32[16,64,128]{2,1,0:T(8,128)S(1)} collective-permute-done((f32[16,64,128]{2,1,0:T(8,128)S(1)}, f32[16,64,128]{2,1,0:T(8,128)S(1)}, u32[]{:S(2)}, u32[]{:S(2)}) %collective-permute-start) | collective-permute-done | bytes 524320 | tf_op jit(solution)/shard_map/ppermute | solution.py:273
  6.5 0.1 add.6
  6.5 22.9 %all_to_all.20.terms_ref = f32[16,64,128]{2,1,0:T(8,128)S(1)} all-to-all(f32[16,64,128]{2,1,0:T(8,128)S(1)} %add.6), channel_id=1, replica_groups=mesh['z_hi'=4,'y'=4,'z_lo'=4,'x'=4,'core'=2] {'z_lo','x'}, dimensions={0} | all-to-all | bytes 1048576 | tf_op jit(solution)/shard_map/all_to_all | solution.py:32
  29.4 0.0 copy-done.5
  29.4 0.6 sketches.1
  30.0 31.1 %all_to_all.21 = f32[64,4,128]{2,1,0:T(4,128)S(1)} all-to-all(f32[64,4,128]{2,1,0:T(4,128)S(1)} %sketches.1), channel_id=1, replica_groups=mesh['z_hi'=4,'y'=4,'z_lo'=4,'x'=4,'core'=2] {'z_hi','z_lo','x'}, dimensions={0} | all-to-all | bytes 262144 | tf_op jit(solution)/shard_map/all_to_all | solution.py:32
  61.1 0.9 broadcast_in_dim.13
  61.9 4.5 %all-to-all-start.2 = ((f32[4,4,64,128]{3,2,1,0:T(8,128)}), f32[4,4,64,128]{3,2,1,0:T(8,128)S(1)}, u32[]{:S(2)}, u32[]{:S(2)}) async-start(f32[4,4,64,128]{3,2,1,0:T(8,128)} %broadcast_in_dim.13), calls=%async_computation.2 | async-start | bytes 1048576 | tf_op jit(solution)/shard_map/all_to_all | solution.py:32
  66.4 1.9 %collective-permute-start.1 = (f32[64,128]{1,0:T(8,128)S(1)}, f32[64,128]{1,0:T(8,128)S(1)}, u32[]{:S(2)}, u32[]{:S(2)}) collective-permute-start(f32[64,128]{1,0:T(8,128)S(1)} %dynamic-slice_bitcast_fusion.own_ref), channel_id=1, source_target_pairs={{0,1},{1,0},{2,3},{3,2},{4,5},{5,4},{6,7},{7,6},{8,9},{9,8},{10,11... | collective-permute-start | bytes 98312 | tf_op jit(solution)/shard_map/ppermute | solution.py:279
  68.3 1.2 %collective-permute-done.1.other_ref = f32[64,128]{1,0:T(8,128)S(1)} collective-permute-done((f32[64,128]{1,0:T(8,128)S(1)}, f32[64,128]{1,0:T(8,128)S(1)}, u32[]{:S(2)}, u32[]{:S(2)}) %collective-permute-start.1) | collective-permute-done | bytes 32800 | tf_op jit(solution)/shard_map/ppermute | solution.py:279
  69.5 5.0 %all-to-all-done.2 = f32[4,4,64,128]{3,2,1,0:T(8,128)S(1)} async-done(((f32[4,4,64,128]{3,2,1,0:T(8,128)}), f32[4,4,64,128]{3,2,1,0:T(8,128)S(1)}, u32[]{:S(2)}, u32[]{:S(2)}) %all-to-all-start.2) | async-done | bytes 524320 | tf_op jit(solution)/shard_map/all_to_all | solution.py:32
  74.5 0.7 gram.1
  75.2 12.0 %all_to_all.22.terms_ref = f32[16,16,128]{2,1,0:T(8,128)S(1)} all-to-all(f32[16,16,128]{2,1,0:T(8,128)S(1)} %gram.1), channel_id=1, replica_groups=mesh['z_hi'=4,'y'=4,'z_lo'=4,'x'=4,'core'=2] {'z_lo','x'}, dimensions={0} | all-to-all | bytes 262144 | tf_op jit(solution)/shard_map/all_to_all | solution.py:32
  87.2 0.9 finish.1
  (5 shorter events, 0.0 us)
Async XLA Ops:
  0.0 4.6 %copy-start = (bf16[64,32,896]{2,1,0:T(8,128)(2,1)S(1)}, bf16[64,32,896]{2,1,0:T(8,128)(2,1)}, u32[]{:S(2)}) copy-start(bf16[64,32,896]{2,1,0:T(8,128)(2,1)} %param.6) | copy-start | bytes 11010052
  0.0 4.6 %copy-start.1 = (bf16[64,32,256]{2,1,0:T(8,128)(2,1)S(1)}, bf16[64,32,256]{2,1,0:T(8,128)(2,1)}, u32[]{:S(2)}) copy-start(bf16[64,32,256]{2,1,0:T(8,128)(2,1)} %param.7) | copy-start | bytes 3145732
  0.0 4.6 %copy-start.2 = (bf16[896,64]{0,1:T(8,128)(2,1)S(1)}, bf16[896,64]{0,1:T(8,128)(2,1)}, u32[]{:S(2)}) copy-start(bf16[896,64]{0,1:T(8,128)(2,1)} %param.8) | copy-start | bytes 344068
  0.0 4.6 %copy-start.3 = (bf16[256,64]{0,1:T(8,128)(2,1)S(1)}, bf16[256,64]{0,1:T(8,128)(2,1)}, u32[]{:S(2)}) copy-start(bf16[256,64]{0,1:T(8,128)(2,1)} %param.9) | copy-start | bytes 98308
  2.6 26.7 %copy-start.5 = (s32[64]{0:T(128)S(1)}, s32[64]{0:T(128)}, u32[]{:S(2)}) copy-start(s32[64]{0:T(128)} %param.10) | copy-start | bytes 772
  2.6 3.8 %collective-permute-start = (f32[16,64,128]{2,1,0:T(8,128)S(1)}, f32[16,64,128]{2,1,0:T(8,128)S(1)}, u32[]{:S(2)}, u32[]{:S(2)}) collective-permute-start(f32[16,64,128]{2,1,0:T(8,128)S(1)} %project.1), channel_id=1, source_target_pairs={{0,1},{1,0},{2,3},{3,2},{4,5},{5,4},{6,7},{7,6},{8,9},{9,8},{10,11... | collective-permute-start | bytes 1572872 | tf_op jit(solution)/shard_map/ppermute | solution.py:273
  5.4 81.7 %copy-start.4 = (s32[16]{0:T(128)S(1)}, s32[16]{0:T(128)}, u32[]{:S(2)}) copy-start(s32[16]{0:T(128)} %param.11) | copy-start | bytes 196
  61.9 12.5 %all-to-all-start.2 = ((f32[4,4,64,128]{3,2,1,0:T(8,128)}), f32[4,4,64,128]{3,2,1,0:T(8,128)S(1)}, u32[]{:S(2)}, u32[]{:S(2)}) async-start(f32[4,4,64,128]{3,2,1,0:T(8,128)} %broadcast_in_dim.13), calls=%async_computation.2 | async-start | bytes 1048576 | tf_op jit(solution)/shard_map/all_to_all | solution.py:32
  66.4 3.1 %collective-permute-start.1 = (f32[64,128]{1,0:T(8,128)S(1)}, f32[64,128]{1,0:T(8,128)S(1)}, u32[]{:S(2)}, u32[]{:S(2)}) collective-permute-start(f32[64,128]{1,0:T(8,128)S(1)} %dynamic-slice_bitcast_fusion.own_ref), channel_id=1, source_target_pairs={{0,1},{1,0},{2,3},{3,2},{4,5},{5,4},{6,7},{7,6},{8,9},{9,8},{10,11... | collective-permute-start | bytes 98312 | tf_op jit(solution)/shard_map/ppermute | solution.py:279

commit v5 on v4

--- a/solution.py
+++ b/solution.py
@@ -239,10 +239,12 @@
     hit = row % n_z * n_y + row // n_z == col
     live = jnp.sum(jnp.where(hit, jnp.broadcast_to(same, (blocks, blocks)), 0.0), axis=1, keepdims=True)
     total = jnp.where(live > 0.5, total, 0.0)
+    halves = (total[:, :seqs], total[:, seqs:])
     for y in range(n_y):
         for z in range(n_z):
-            line = total[y * n_z + z : y * n_z + z + 1]
-            out_ref[z * n_y + y] = jnp.concatenate([line[:, :seqs], line[:, seqs:]], axis=0)
+            line = y * n_z + z
+            for s in range(2):
+                out_ref[z * n_y + y, s : s + 1, :] = halves[s][line : line + 1]
 
 
 def finish(tasks, terms):

time: 88.3 us -> 88.3 us (level)
  no operation moved by 1% of the time
where the time goes in v5:
time: 88.3 us; the launch traced here: 88 us
  blocking collectives  66 us (75%)
  starting transfers between devices  8.29 us (9%)
  waiting for transfers between devices  7.16 us (8%)
  Pallas kernels  5.62 us (6%)
    all_to_all x3, blocking collectives, exchange(): return lax.all_to_all(value, axes, 0, 0, tiled=True)  66 us
    all_to_all x1, waiting for transfers between devices, exchange(): return lax.all_to_all(value, axes, 0, 0, tiled=True)  4.99 us
    all_to_all x1, starting transfers between devices, exchange(): return lax.all_to_all(value, axes, 0, 0, tiled=True)  4.47 us
    pallas_call x1, Pallas kernels, project(): pl.pallas_call(project_kernel, in_specs=[HBM, HBM, HBM, HBM], out_specs=V...  2.61 us
    ppermute x1, starting transfers between devices, body(): mine = add(keep, lax.ppermute(send, 'core', [(0, 1), (1, 0)]))  1.92 us
    ppermute x1, starting transfers between devices, body(): other = lax.ppermute(mine, 'core', [(0, 1), (1, 0)])  1.91 us
  transfers between devices with their start and end apart: 3, of which 3 were waited for; matrix products, arithmetic and copies ran while one was open for 0% of the time, Pallas kernels for 1%

profile of v5, /device:TPU:2, one launch (start us, length us, event | category | flops | bytes accessed | tf_op | source)
XLA Modules:
  0.0 88.0 jit_solution(9402465335281225155)
XLA Ops:
  0.0 0.0 copy-start.3
  0.0 2.6 %project.1 = f32[16,64,128]{2,1,0:T(8,128)S(1)} custom-call(bf16[16,2,64,896]{3,2,1,0:T(8,128)(2,1)} %bitcast.11, bf16[16,2,64,256]{3,2,1,0:T(8,128)(2,1)} %bitcast.13, bf16[64,896]{1,0:T(8,128)(2,1)} %bitcast.16, bf16[64,256]{1,0:T(8,128)(2,1)} %bitcast.18), custom_call_target="tpu_custom_call" | custom-call | flops 150994944 | bytes 2883584 | tf_op jit(solution)/shard_map/project/pallas_call | solution.py:80
  2.6 0.0 copy-start.5
  2.6 1.9 %collective-permute-start = (f32[16,64,128]{2,1,0:T(8,128)S(1)}, f32[16,64,128]{2,1,0:T(8,128)S(1)}, u32[]{:S(2)}, u32[]{:S(2)}) collective-permute-start(f32[16,64,128]{2,1,0:T(8,128)S(1)} %project.1), channel_id=1, source_target_pairs={{0,1},{1,0},{2,3},{3,2},{4,5},{5,4},{6,7},{7,6},{8,9},{9,8},{10,11... | collective-permute-start | bytes 1572872 | tf_op jit(solution)/shard_map/ppermute | solution.py:275
  4.6 0.0 copy-done
  4.6 0.0 copy-done.1
  4.6 0.0 copy-done.2
  4.6 0.0 copy-done.3
  4.6 0.8 project_rest.1.left_ref
  5.4 0.0 copy-start.4
  5.5 1.0 %collective-permute-done.right_ref = f32[16,64,128]{2,1,0:T(8,128)S(1)} collective-permute-done((f32[16,64,128]{2,1,0:T(8,128)S(1)}, f32[16,64,128]{2,1,0:T(8,128)S(1)}, u32[]{:S(2)}, u32[]{:S(2)}) %collective-permute-start) | collective-permute-done | bytes 524320 | tf_op jit(solution)/shard_map/ppermute | solution.py:275
  6.5 0.1 add.6
  6.5 22.9 %all_to_all.20.terms_ref = f32[16,64,128]{2,1,0:T(8,128)S(1)} all-to-all(f32[16,64,128]{2,1,0:T(8,128)S(1)} %add.6), channel_id=1, replica_groups=mesh['z_hi'=4,'y'=4,'z_lo'=4,'x'=4,'core'=2] {'z_lo','x'}, dimensions={0} | all-to-all | bytes 1048576 | tf_op jit(solution)/shard_map/all_to_all | solution.py:32
  29.4 0.0 copy-done.5
  29.4 0.6 sketches.1
  30.0 31.1 %all_to_all.21 = f32[64,4,128]{2,1,0:T(4,128)S(1)} all-to-all(f32[64,4,128]{2,1,0:T(4,128)S(1)} %sketches.1), channel_id=1, replica_groups=mesh['z_hi'=4,'y'=4,'z_lo'=4,'x'=4,'core'=2] {'z_hi','z_lo','x'}, dimensions={0} | all-to-all | bytes 262144 | tf_op jit(solution)/shard_map/all_to_all | solution.py:32
  61.1 0.9 broadcast_in_dim.13
  61.9 4.5 %all-to-all-start.2 = ((f32[4,4,64,128]{3,2,1,0:T(8,128)}), f32[4,4,64,128]{3,2,1,0:T(8,128)S(1)}, u32[]{:S(2)}, u32[]{:S(2)}) async-start(f32[4,4,64,128]{3,2,1,0:T(8,128)} %broadcast_in_dim.13), calls=%async_computation.2 | async-start | bytes 1048576 | tf_op jit(solution)/shard_map/all_to_all | solution.py:32
  66.4 1.9 %collective-permute-start.1 = (f32[64,128]{1,0:T(8,128)S(1)}, f32[64,128]{1,0:T(8,128)S(1)}, u32[]{:S(2)}, u32[]{:S(2)}) collective-permute-start(f32[64,128]{1,0:T(8,128)S(1)} %dynamic-slice_bitcast_fusion.own_ref), channel_id=1, source_target_pairs={{0,1},{1,0},{2,3},{3,2},{4,5},{5,4},{6,7},{7,6},{8,9},{9,8},{10,11... | collective-permute-start | bytes 98312 | tf_op jit(solution)/shard_map/ppermute | solution.py:281
  68.3 1.2 %collective-permute-done.1.other_ref = f32[64,128]{1,0:T(8,128)S(1)} collective-permute-done((f32[64,128]{1,0:T(8,128)S(1)}, f32[64,128]{1,0:T(8,128)S(1)}, u32[]{:S(2)}, u32[]{:S(2)}) %collective-permute-start.1) | collective-permute-done | bytes 32800 | tf_op jit(solution)/shard_map/ppermute | solution.py:281
  69.5 5.0 %all-to-all-done.2 = f32[4,4,64,128]{3,2,1,0:T(8,128)S(1)} async-done(((f32[4,4,64,128]{3,2,1,0:T(8,128)}), f32[4,4,64,128]{3,2,1,0:T(8,128)S(1)}, u32[]{:S(2)}, u32[]{:S(2)}) %all-to-all-start.2) | async-done | bytes 524320 | tf_op jit(solution)/shard_map/all_to_all | solution.py:32
  74.5 0.7 gram.1
  75.2 12.0 %all_to_all.22.terms_ref = f32[16,16,128]{2,1,0:T(8,128)S(1)} all-to-all(f32[16,16,128]{2,1,0:T(8,128)S(1)} %gram.1), channel_id=1, replica_groups=mesh['z_hi'=4,'y'=4,'z_lo'=4,'x'=4,'core'=2] {'z_lo','x'}, dimensions={0} | all-to-all | bytes 262144 | tf_op jit(solution)/shard_map/all_to_all | solution.py:32
  87.2 0.8 finish.1
  (5 shorter events, 0.0 us)
Async XLA Ops:
  0.0 4.6 %copy-start = (bf16[64,32,896]{2,1,0:T(8,128)(2,1)S(1)}, bf16[64,32,896]{2,1,0:T(8,128)(2,1)}, u32[]{:S(2)}) copy-start(bf16[64,32,896]{2,1,0:T(8,128)(2,1)} %param.6) | copy-start | bytes 11010052
  0.0 4.6 %copy-start.1 = (bf16[64,32,256]{2,1,0:T(8,128)(2,1)S(1)}, bf16[64,32,256]{2,1,0:T(8,128)(2,1)}, u32[]{:S(2)}) copy-start(bf16[64,32,256]{2,1,0:T(8,128)(2,1)} %param.7) | copy-start | bytes 3145732
  0.0 4.6 %copy-start.2 = (bf16[896,64]{0,1:T(8,128)(2,1)S(1)}, bf16[896,64]{0,1:T(8,128)(2,1)}, u32[]{:S(2)}) copy-start(bf16[896,64]{0,1:T(8,128)(2,1)} %param.8) | copy-start | bytes 344068
  0.0 4.6 %copy-start.3 = (bf16[256,64]{0,1:T(8,128)(2,1)S(1)}, bf16[256,64]{0,1:T(8,128)(2,1)}, u32[]{:S(2)}) copy-start(bf16[256,64]{0,1:T(8,128)(2,1)} %param.9) | copy-start | bytes 98308
  2.6 26.7 %copy-start.5 = (s32[64]{0:T(128)S(1)}, s32[64]{0:T(128)}, u32[]{:S(2)}) copy-start(s32[64]{0:T(128)} %param.10) | copy-start | bytes 772
  2.6 3.8 %collective-permute-start = (f32[16,64,128]{2,1,0:T(8,128)S(1)}, f32[16,64,128]{2,1,0:T(8,128)S(1)}, u32[]{:S(2)}, u32[]{:S(2)}) collective-permute-start(f32[16,64,128]{2,1,0:T(8,128)S(1)} %project.1), channel_id=1, source_target_pairs={{0,1},{1,0},{2,3},{3,2},{4,5},{5,4},{6,7},{7,6},{8,9},{9,8},{10,11... | collective-permute-start | bytes 1572872 | tf_op jit(solution)/shard_map/ppermute | solution.py:275
  5.4 81.7 %copy-start.4 = (s32[16]{0:T(128)S(1)}, s32[16]{0:T(128)}, u32[]{:S(2)}) copy-start(s32[16]{0:T(128)} %param.11) | copy-start | bytes 196
  61.9 12.5 %all-to-all-start.2 = ((f32[4,4,64,128]{3,2,1,0:T(8,128)}), f32[4,4,64,128]{3,2,1,0:T(8,128)S(1)}, u32[]{:S(2)}, u32[]{:S(2)}) async-start(f32[4,4,64,128]{3,2,1,0:T(8,128)} %broadcast_in_dim.13), calls=%async_computation.2 | async-start | bytes 1048576 | tf_op jit(solution)/shard_map/all_to_all | solution.py:32
  66.4 3.1 %collective-permute-start.1 = (f32[64,128]{1,0:T(8,128)S(1)}, f32[64,128]{1,0:T(8,128)S(1)}, u32[]{:S(2)}, u32[]{:S(2)}) collective-permute-start(f32[64,128]{1,0:T(8,128)S(1)} %dynamic-slice_bitcast_fusion.own_ref), channel_id=1, source_target_pairs={{0,1},{1,0},{2,3},{3,2},{4,5},{5,4},{6,7},{7,6},{8,9},{9,8},{10,11... | collective-permute-start | bytes 98312 | tf_op jit(solution)/shard_map/ppermute | solution.py:281
